TPU v7x, 512 devices: a whole 4x4x16 slice. The times are simulated.
512 devices in a mesh: slab: 128 (over y, z, core), sub: 4 (over x).
Axes of the slice: x: 4, y: 4, z: 16, core: 2. Of those that a mesh axis runs over, the one named last changes fastest.
Arguments:
- mode_shapes: bfloat16 [32, 6, 1024, 512], P(None, None, 'slab', 'sub')
- span_stiff: float32 [6, 1024, 512], P(None, 'slab', 'sub'), may hold values from -4 to 4
- chord_stiff: float32 [6, 1024, 512], P(None, 'slab', 'sub'), may hold values from -4 to 4
- span_geo: float32 [1024, 512], P('slab', 'sub'), may hold values from 0.2 to 2
- chord_geo: float32 [1024, 512], P('slab', 'sub'), may hold values from 0.2 to 2
- ground: float32 [6, 1024, 512], P(None, 'slab', 'sub'), may hold values from 0.2 to 2
- chord_len: int32 [1024], replicated, may hold values from 192 to 512, as said below
Outputs:
- adjoint: float32 [32, 6, 1024, 512], P(None, None, 'slab', 'sub')
- residual: float32 [32, 6, 1024, 512], P(None, None, 'slab', 'sub')
Inputs may be any that keep to these rules, and one draw needn't show every extreme that they name: chord_len[0] = 512.
All inputs are finite; a program needn't handle non-finite values.
Results may differ from a plain program's by a relative error of at most 0.0003.
Values sent between devices are 32-bit elements; how exact they have to be, the bound alone decides.
A program may use at most 64 MiB of HBM per device.

v0:
```python
import jax
import jax.numpy as jnp
from jax import lax
from jax.sharding import PartitionSpec as P

ITERS = 2


def from_behind(value, axis, steps):
    count = lax.axis_size(axis)
    initial, last = (max(0, -steps), min(count, count - steps))
    return lax.ppermute(value, axis, [(source, source + steps) for source in range(initial, last)])


def factor_blocks(blocks):
    count = len(blocks)
    factor = [[None] * count for i in range(count)]
    inverse = [None] * count
    for j in range(count):
        running = blocks[j][j]
        for k in range(j):
            running = running - factor[j][k] * factor[j][k]
        diag_root = jnp.sqrt(running)
        factor[j][j] = diag_root
        inverse[j] = 1.0 / diag_root
        for i in range(j + 1, count):
            running = blocks[i][j]
            for k in range(j):
                running = running - factor[i][k] * factor[j][k]
            factor[i][j] = running * inverse[j]
    return (factor, inverse)


def solve_blocks(factor, inverse, vector):
    count = len(inverse)
    forward = []
    for i in range(count):
        running = vector[:, i]
        for j in range(i):
            running = running - factor[i][j][None] * forward[j]
        forward.append(running * inverse[i][None])
    backward = [None] * count
    for i in reversed(range(count)):
        running = forward[i]
        for j in range(i + 1, count):
            running = running - factor[j][i][None] * backward[j]
        backward[i] = running * inverse[i][None]
    return jnp.stack(backward, axis=1)


def neighbours_ahead(field):
    next_station = from_behind(field[:, :, :1, :], "slab", -1)
    next_column = from_behind(field[:, :, :, :1], "sub", -1)
    span_next = jnp.concatenate([field[:, :, 1:, :], next_station], axis=2)
    chord_next = jnp.concatenate([field[:, :, :, 1:], next_column], axis=3)
    return (span_next, chord_next)


def forces_behind(span_forces, chord_forces):
    from_span = from_behind(span_forces[:, :, -1:, :], "slab", 1)
    from_chord = from_behind(chord_forces[:, :, :, -1:], "sub", 1)
    span_part = jnp.concatenate([from_span, span_forces[:, :, :-1, :]], axis=2)
    chord_part = jnp.concatenate([from_chord, chord_forces[:, :, :, :-1]], axis=3)
    return span_part + chord_part


def edge_forces(stiffness, jump, live_mask):
    strain = jnp.sum(stiffness[None] * jump, axis=1) * live_mask[None]
    return stiffness[None] * strain[:, None]


def operate_sent(field, span_stiff, chord_stiff, span_live, chord_live, ground):
    span_next, chord_next = neighbours_ahead(field)
    span_forces = edge_forces(span_stiff, span_next - field, span_live)
    chord_forces = edge_forces(chord_stiff, chord_next - field, chord_live)
    return (
        ground[None] * field - span_forces - chord_forces + forces_behind(span_forces, chord_forces)
    )


def inner_rz(first, second):
    return lax.psum(jnp.sum(first * second, axis=(1, 2, 3)), ("slab", "sub"))


def inner_pq(first, second):
    return lax.psum(jnp.sum(first * second, axis=(1, 2, 3)), ("slab", "sub"))


def body(mode_shapes, span_stiff, chord_stiff, span_geo, chord_geo, ground, chord_len):
    count = ground.shape[0]
    stations = ground.shape[1]
    columns = ground.shape[2]
    row_start = lax.axis_index("slab") * stations
    col_start = lax.axis_index("sub") * columns
    padded_len = jnp.concatenate(
        [jnp.zeros((1,), jnp.int32), chord_len, jnp.zeros((2,), jnp.int32)]
    )
    window = lax.dynamic_slice_in_dim(padded_len, row_start, stations + 2)
    col_global = (col_start + jnp.arange(columns, dtype=jnp.int32))[None, :]
    span_mask_wide = ((col_global < window[:-1, None]) & (col_global < window[1:, None])).astype(
        jnp.float32
    )
    col_wide = (col_start - 1 + jnp.arange(columns + 1, dtype=jnp.int32))[None, :]
    own_len = window[1 : stations + 1, None]
    chord_mask_wide = ((col_wide + 1 < own_len) & (col_wide >= 0)).astype(jnp.float32)
    span_live = span_mask_wide[1:]
    chord_live = chord_mask_wide[:, 1:]
    ghost_span = from_behind(span_stiff[:, stations - 1 :, :], "slab", 1)
    ghost_chord = from_behind(chord_stiff[:, :, columns - 1 :], "sub", 1)
    span_wide = jnp.concatenate([ghost_span, span_stiff], axis=1)
    chord_wide = jnp.concatenate([ghost_chord, chord_stiff], axis=2)
    blocks = []
    for i in range(count):
        block_row = []
        for j in range(count):
            span_pair = span_wide[i] * span_wide[j] * span_mask_wide
            chord_pair = chord_wide[i] * chord_wide[j] * chord_mask_wide
            entry = span_pair[1:] + span_pair[:-1] + chord_pair[:, 1:] + chord_pair[:, :-1]
            if i == j:
                entry = entry + ground[i]
            block_row.append(entry)
        blocks.append(block_row)
    factor, inverse = factor_blocks(blocks)
    mode_field = mode_shapes.astype(jnp.float32)
    span_next, chord_next = neighbours_ahead(mode_field)
    span_jump = span_next - mode_field
    chord_jump = chord_next - mode_field
    span_weight = jnp.sum(span_jump * span_jump, axis=1) * (span_geo * span_live)[None]
    chord_weight = jnp.sum(chord_jump * chord_jump, axis=1) * (chord_geo * chord_live)[None]
    span_load = span_stiff[None] * span_weight[:, None]
    chord_load = chord_stiff[None] * chord_weight[:, None]
    load = forces_behind(span_load, chord_load) - span_load - chord_load
    solution = jnp.zeros_like(load)
    residual = load
    precond = solve_blocks(factor, inverse, residual)
    direction = precond
    precond_norm = inner_rz(residual, precond)
    for step in range(ITERS):
        image = operate_sent(direction, span_stiff, chord_stiff, span_live, chord_live, ground)
        step_size = precond_norm / inner_pq(direction, image)
        solution = solution + step_size[:, None, None, None] * direction
        residual = residual - step_size[:, None, None, None] * image
        if step + 1 < ITERS:
            precond = solve_blocks(factor, inverse, residual)
            norm_next = inner_rz(residual, precond)
            direction = precond + (norm_next / precond_norm)[:, None, None, None] * direction
            precond_norm = norm_next
    return (solution, residual)


def solution(mesh):
    return jax.shard_map(
        body,
        mesh=mesh,
        in_specs=(
            P(None, None, "slab", "sub"),
            P(None, "slab", "sub"),
            P(None, "slab", "sub"),
            P("slab", "sub"),
            P("slab", "sub"),
            P(None, "slab", "sub"),
            P(),
        ),
        out_specs=(P(None, None, "slab", "sub"), P(None, None, "slab", "sub")),
        check_vma=False,
    )
```

profile of v0, /device:TPU:1, one launch (start us, length us, event | category | flops | bytes accessed | tf_op | source)
XLA Modules:
  0.0 413.0 jit_solution(10485907390977975643)
XLA Ops:
  0.6 0.7 slice.527
  1.4 4.9 %collective-permute-start.4 = (f32[6,1,128]{2,1,0:T(1,128)S(1)}, f32[6,1,128]{2,1,0:T(1,128)S(1)}, u32[]{:S(2)}, u32[]{:S(2)}) collective-permute-start(f32[6,1,128]{2,1,0:T(1,128)S(1)} %slice.527), channel_id=1, source_target_pairs={{0,4},{4,8},{8,12},{12,16},{16,20},{20,24},{24,28},{28,32},{32,36}... | collective-permute-start | bytes 9224 | tf_op jit(solution)/shard_map/ppermute | solution.py:12
  6.3 0.8 slice.531
  7.1 3.1 collective-permute-start.5
  10.2 1.1 copy_convert_fusion
  11.7 1.3 collective-permute-start.2
  13.0 3.3 collective-permute-start
  22.5 0.7 copy-done.6
  23.4 0.7 fusion.94
  24.1 0.7 fusion.78
  25.3 0.7 fusion.70
  27.8 2.2 collective-permute-start.1
  30.8 4.0 collective-permute-start.3
  34.9 0.9 collective-permute-done.3
  36.2 1.3 fusion.3
  39.2 1.3 collective-permute-start.7
  40.5 3.8 collective-permute-start.6
  44.4 0.9 slice.780
  45.9 0.8 collective-permute-done.6
  46.7 1.6 fusion.9
  48.4 0.7 slice.784
  49.1 2.1 collective-permute-start.8
  51.3 1.2 slice.786
  52.5 2.1 copy.16
  54.6 4.4 %collective-permute-start.9 = (f32[32,6,8,1]{0,2,3,1:T(8,128)}, f32[32,6,8,1]{0,2,3,1:T(8,128)}, u32[]{:S(2)}, u32[]{:S(2)}) collective-permute-start(f32[32,6,8,1]{0,2,3,1:T(8,128)} %copy.16), channel_id=1, source_target_pairs={{0,1},{1,2},{2,3},{4,5},{5,6},{6,7},{8,9},{9,10},{10,11},{12,13},{... | collective-permute-start | bytes 18440 | tf_op jit(solution)/shard_map/ppermute | solution.py:12
  59.5 2.0 copy.17
  61.5 2.6 multiply_reduce_fusion.2
  64.1 112.9 %all-reduce = (f32[32]{0:T(128)S(1)}, f32[32]{0:T(128)S(1)}) all-reduce(f32[32]{0:T(128)S(1)} %get-tuple-element.7, f32[32]{0:T(128)S(1)} %get-tuple-element.6), channel_id=1, replica_groups=mesh['slab'=128,'sub'=4] {'slab','sub'}, use_global_device_ids=true, to_apply=%region_3.0 | all-reduce | flops 64 | bytes 512 | tf_op jit(solution)/shard_map/psum | solution.py:82
  177.6 1.3 multiply_subtract_fusion.1
  180.0 98.7 %psum.30 = f32[32]{0:T(128)S(1)} all-reduce(f32[32]{0:T(128)S(1)} %multiply_reduce_fusion.1), channel_id=1, replica_groups=mesh['slab'=128,'sub'=4] {'slab','sub'}, use_global_device_ids=true, to_apply=%region_9.0 | all-reduce | flops 32 | bytes 256 | tf_op jit(solution)/shard_map/psum | solution.py:82
  278.9 2.6 collective-permute-start.10
  281.8 1.3 collective-permute-start.11
  283.1 0.9 slice.794
  284.3 2.3 collective-permute-done.11
  286.6 1.2 copy.19
  287.9 1.8 fusion.14
  290.5 0.7 slice.798
  291.4 4.5 %collective-permute-start.12 = (f32[32,6,1,128]{3,0,2,1:T(8,128)}, f32[32,6,1,128]{3,0,2,1:T(8,128)}, u32[]{:S(2)}, u32[]{:S(2)}) collective-permute-start(f32[32,6,1,128]{3,0,2,1:T(8,128)} %slice.798), channel_id=1, source_target_pairs={{0,4},{4,8},{8,12},{12,16},{16,20},{20,24},{24,28},{28,32},{32,36}... | collective-permute-start | bytes 294920 | tf_op jit(solution)/shard_map/ppermute | solution.py:12
  296.0 1.2 slice.800
  297.1 1.5 copy.20
  298.6 2.9 collective-permute-start.13
  301.5 2.0 slice.799
  303.5 1.2 copy.21
  304.7 2.7 multiply_reduce_fusion
  307.5 100.6 %psum.31 = f32[32]{0:T(128)S(1)} all-reduce(f32[32]{0:T(128)S(1)} %get-tuple-element.14), channel_id=1, replica_groups=mesh['slab'=128,'sub'=4] {'slab','sub'}, use_global_device_ids=true, to_apply=%region_13.0 | all-reduce | flops 32 | bytes 256 | tf_op jit(solution)/shard_map/psum | solution.py:86
  408.8 1.5 multiply_subtract_fusion
  410.3 1.3 copy.23
  411.7 1.3 copy.22
  (143 shorter events, 17.3 us)
Async XLA Ops:
  1.4 20.2 %collective-permute-start.4 = (f32[6,1,128]{2,1,0:T(1,128)S(1)}, f32[6,1,128]{2,1,0:T(1,128)S(1)}, u32[]{:S(2)}, u32[]{:S(2)}) collective-permute-start(f32[6,1,128]{2,1,0:T(1,128)S(1)} %slice.527), channel_id=1, source_target_pairs={{0,4},{4,8},{8,12},{12,16},{16,20},{20,24},{24,28},{28,32},{32,36}... | collective-permute-start | bytes 9224 | tf_op jit(solution)/shard_map/ppermute | solution.py:12
  7.1 13.7 %collective-permute-start.5 = (f32[6,8,1]{2,1,0:T(8,128)S(1)}, f32[6,8,1]{2,1,0:T(8,128)S(1)}, u32[]{:S(2)}, u32[]{:S(2)}) collective-permute-start(f32[6,8,1]{2,1,0:T(8,128)S(1)} %slice.531), channel_id=1, source_target_pairs={{0,1},{1,2},{2,3},{4,5},{5,6},{6,7},{8,9},{9,10},{10,11},{12,13},{... | collective-permute-start | bytes 584 | tf_op jit(solution)/shard_map/ppermute | solution.py:12
  11.7 14.3 %collective-permute-start.2 = (f32[32,6,8,1]{0,2,3,1:T(8,128)S(1)}, f32[32,6,8,1]{0,2,3,1:T(8,128)S(1)}, u32[]{:S(2)}, u32[]{:S(2)}) collective-permute-start(f32[32,6,8,1]{0,2,3,1:T(8,128)S(1)} %copy.10), channel_id=1, source_target_pairs={{1,0},{2,1},{3,2},{5,4},{6,5},{7,6},{9,8},{10,9},{11,10},{13,12},{... | collective-permute-start | bytes 18440 | tf_op jit(solution)/shard_map/ppermute | solution.py:12
  13.0 13.4 %collective-permute-start = (f32[32,6,1,128]{3,0,2,1:T(8,128)S(1)}, f32[32,6,1,128]{3,0,2,1:T(8,128)S(1)}, u32[]{:S(2)}, u32[]{:S(2)}) collective-permute-start(f32[32,6,1,128]{3,0,2,1:T(8,128)S(1)} %slice.661), channel_id=1, source_target_pairs={{4,0},{8,4},{12,8},{16,12},{20,16},{24,20},{28,24},{32,28},{36,32}... | collective-permute-start | bytes 294920 | tf_op jit(solution)/shard_map/ppermute | solution.py:12
  16.4 0.7 copy-start.25
  17.2 0.7 copy-start.26
  18.6 0.7 copy-start.27
  19.2 0.6 copy-start.23
  20.6 0.7 copy-start.3
  21.5 0.7 copy-start.4
  21.6 3.2 copy-start.7
  22.4 0.7 copy-start.6
  24.7 0.6 copy-start.19
  26.0 1.0 copy-start.5
  27.0 0.7 copy-start.22
  27.8 7.1 %copy-start = (f32[32,6,8,128]{3,0,2,1:T(8,128)}, f32[32,6,8,128]{3,0,2,1:T(8,128)S(1)}, u32[]{:S(2)}) copy-start(f32[32,6,8,128]{3,0,2,1:T(8,128)S(1)} %broadcast_multiply_fusion.5) | copy-start | bytes 2359300
  27.8 2.3 copy-start.21
  27.8 8.3 %collective-permute-start.1 = (f32[32,6,1,128]{3,0,2,1:T(8,128)S(1)}, f32[32,6,1,128]{3,0,2,1:T(8,128)}, u32[]{:S(2)}, u32[]{:S(2)}) collective-permute-start(f32[32,6,1,128]{3,0,2,1:T(8,128)S(1)} %slice.663), channel_id=1, source_target_pairs={{0,4},{4,8},{8,12},{12,16},{16,20},{20,24},{24,28},{28,32},{32,36}... | collective-permute-start | bytes 294920 | tf_op jit(solution)/shard_map/ppermute | solution.py:12
  30.5 4.4 %copy-start.8 = (f32[8,129]{1,0:T(8,128)S(1)}, f32[8,129]{1,0:T(8,128)}, u32[]{:S(2)}) copy-start(f32[8,129]{1,0:T(8,128)} %copy-done.7) | copy-start | bytes 12388
  30.5 4.4 %copy-start.20 = (f32[8,128]{1,0:T(8,128)S(1)}, f32[8,128]{1,0:T(8,128)}, u32[]{:S(2)}) copy-start(f32[8,128]{1,0:T(8,128)} %copy-done.19) | copy-start | bytes 12292
  30.8 4.9 %collective-permute-start.3 = (f32[32,6,8,1]{0,2,3,1:T(8,128)S(1)}, f32[32,6,8,1]{0,2,3,1:T(8,128)S(1)}, u32[]{:S(2)}, u32[]{:S(2)}) collective-permute-start(f32[32,6,8,1]{0,2,3,1:T(8,128)S(1)} %copy.12), channel_id=1, source_target_pairs={{0,1},{1,2},{2,3},{4,5},{5,6},{6,7},{8,9},{9,10},{10,11},{12,13},{... | collective-permute-start | bytes 18440 | tf_op jit(solution)/shard_map/ppermute | solution.py:12
  34.9 1.2 slice-start
  36.1 1.3 copy-start.15
  37.4 0.7 copy-start.13
  37.4 0.7 copy-start.11
  38.8 5.5 %copy-start.24 = (pred[9,128]{1,0:T(8,128)(4,1)S(1)}, pred[9,128]{1,0:T(8,128)(4,1)}, u32[]{:S(2)}) copy-start(pred[9,128]{1,0:T(8,128)(4,1)} %copy-done.23) | copy-start | bytes 3460
  39.2 6.4 %collective-permute-start.7 = (f32[32,6,8,1]{0,2,3,1:T(8,128)S(1)}, f32[32,6,8,1]{0,2,3,1:T(8,128)S(1)}, u32[]{:S(2)}, u32[]{:S(2)}) collective-permute-start(f32[32,6,8,1]{0,2,3,1:T(8,128)S(1)} %copy.14), channel_id=1, source_target_pairs={{1,0},{2,1},{3,2},{5,4},{6,5},{7,6},{9,8},{10,9},{11,10},{13,12},{... | collective-permute-start | bytes 18440 | tf_op jit(solution)/shard_map/ppermute | solution.py:12
  40.5 6.2 %collective-permute-start.6 = (f32[32,6,1,128]{3,0,2,1:T(8,128)S(1)}, f32[32,6,1,128]{3,0,2,1:T(8,128)S(1)}, u32[]{:S(2)}, u32[]{:S(2)}) collective-permute-start(f32[32,6,1,128]{3,0,2,1:T(8,128)S(1)} %slice.781), channel_id=1, source_target_pairs={{4,0},{8,4},{12,8},{16,12},{20,16},{24,20},{28,24},{32,28},{36,32}... | collective-permute-start | bytes 294920 | tf_op jit(solution)/shard_map/ppermute | solution.py:12
  44.4 3.9 copy-start.17
  48.4 10.6 %copy-start.1 = (f32[32,6,8,128]{3,0,2,1:T(8,128)}, f32[32,6,8,128]{3,0,2,1:T(8,128)S(1)}, u32[]{:S(2)}) copy-start(f32[32,6,8,128]{3,0,2,1:T(8,128)S(1)} %broadcast_multiply_fusion.3) | copy-start | bytes 2359300
  48.4 2.8 copy-start.9
  49.1 12.4 %collective-permute-start.8 = (f32[32,6,1,128]{3,0,2,1:T(8,128)}, f32[32,6,1,128]{3,0,2,1:T(8,128)}, u32[]{:S(2)}, u32[]{:S(2)}) collective-permute-start(f32[32,6,1,128]{3,0,2,1:T(8,128)} %slice.784), channel_id=1, source_target_pairs={{0,4},{4,8},{8,12},{12,16},{16,20},{20,24},{24,28},{28,32},{32,36}... | collective-permute-start | bytes 294920 | tf_op jit(solution)/shard_map/ppermute | solution.py:12
  54.6 4.9 %collective-permute-start.9 = (f32[32,6,8,1]{0,2,3,1:T(8,128)}, f32[32,6,8,1]{0,2,3,1:T(8,128)}, u32[]{:S(2)}, u32[]{:S(2)}) collective-permute-start(f32[32,6,8,1]{0,2,3,1:T(8,128)} %copy.16), channel_id=1, source_target_pairs={{0,1},{1,2},{2,3},{4,5},{5,6},{6,7},{8,9},{9,10},{10,11},{12,13},{... | collective-permute-start | bytes 18440 | tf_op jit(solution)/shard_map/ppermute | solution.py:12
  59.0 2.5 slice-start.1
  177.0 0.6 copy-start.28
  177.6 1.4 copy-start.12
  177.6 1.4 copy-start.14
  177.6 1.4 copy-start.16
  278.9 9.0 %collective-permute-start.10 = (f32[32,6,1,128]{3,0,2,1:T(8,128)S(1)}, f32[32,6,1,128]{3,0,2,1:T(8,128)S(1)}, u32[]{:S(2)}, u32[]{:S(2)}) collective-permute-start(f32[32,6,1,128]{3,0,2,1:T(8,128)S(1)} %slice.795), channel_id=1, source_target_pairs={{4,0},{8,4},{12,8},{16,12},{20,16},{24,20},{28,24},{32,28},{36,32}... | collective-permute-start | bytes 294920 | tf_op jit(solution)/shard_map/ppermute | solution.py:12
  281.8 4.8 %collective-permute-start.11 = (f32[32,6,8,1]{0,2,3,1:T(8,128)S(1)}, f32[32,6,8,1]{0,2,3,1:T(8,128)S(1)}, u32[]{:S(2)}, u32[]{:S(2)}) collective-permute-start(f32[32,6,8,1]{0,2,3,1:T(8,128)S(1)} %copy.18), channel_id=1, source_target_pairs={{1,0},{2,1},{3,2},{5,4},{6,5},{7,6},{9,8},{10,9},{11,10},{13,12},{... | collective-permute-start | bytes 18440 | tf_op jit(solution)/shard_map/ppermute | solution.py:12
  287.9 1.8 copy-start.10
  289.7 0.7 copy-start.18
  290.5 0.9 copy-start.2
  291.4 13.3 %collective-permute-start.12 = (f32[32,6,1,128]{3,0,2,1:T(8,128)}, f32[32,6,1,128]{3,0,2,1:T(8,128)}, u32[]{:S(2)}, u32[]{:S(2)}) collective-permute-start(f32[32,6,1,128]{3,0,2,1:T(8,128)} %slice.798), channel_id=1, source_target_pairs={{0,4},{4,8},{8,12},{12,16},{16,20},{20,24},{24,28},{28,32},{32,36}... | collective-permute-start | bytes 294920 | tf_op jit(solution)/shard_map/ppermute | solution.py:12
  298.6 4.9 %collective-permute-start.13 = (f32[32,6,8,1]{0,2,3,1:T(8,128)S(1)}, f32[32,6,8,1]{0,2,3,1:T(8,128)S(1)}, u32[]{:S(2)}, u32[]{:S(2)}) collective-permute-start(f32[32,6,8,1]{0,2,3,1:T(8,128)S(1)} %copy.20), channel_id=1, source_target_pairs={{0,1},{1,2},{2,3},{4,5},{5,6},{6,7},{8,9},{9,10},{10,11},{12,13},{... | collective-permute-start | bytes 18440 | tf_op jit(solution)/shard_map/ppermute | solution.py:12
  408.1 0.7 copy-start.29
where the time goes:
time: 415 us; the launch traced here: 413 us
  blocking collectives  312 us (75%)
  starting transfers between devices  41.7 us (10%)
  local copies, waits for them, and re-layouts  31.7 us (8%)
  other arithmetic  21.5 us (5%)
  waiting for transfers between devices  4.56 us (1%)
    psum x2, blocking collectives, inner_rz(): return lax.psum(jnp.sum(first * second, axis=(1, 2, 3)), ('slab', 'sub'))  212 us
    psum x1, blocking collectives, inner_pq(): return lax.psum(jnp.sum(first * second, axis=(1, 2, 3)), ('slab', 'sub'))  101 us
    ppermute x14, starting transfers between devices, from_behind(): lax.ppermute(value, axis, [(source, source + steps) for source in range(i...  41.7 us
    unnamed x64, local copies, waits for them, and re-layouts  10.6 us
  transfers between devices with their start and end apart: 14, of which 4 were waited for; matrix products, arithmetic and copies ran while one was open for 6% of the time, Pallas kernels for 0%

commit v1 on v0

v1 whole, which is shorter than its diff:
```python
import functools

import jax
import jax.numpy as jnp
from jax import lax
from jax.experimental import pallas as pl
from jax.experimental.pallas import tpu as pltpu
from jax.sharding import PartitionSpec as P

MESH = pl.DeviceIdType.MESH
D = 6
R, C = 8, 128
M = 32
GROUPS = 4
GM = M // GROUPS
UNROLL = 2


def digit_stages(n_slab, n_sub):
    core = 2
    z = 16 if n_slab % 32 == 0 else 1
    y = n_slab // (core * z)
    stages = [[("slab", 1, core), ("sub", 1, n_sub)]]
    if z > 1:
        stages.append([("slab", core, z)])
    if y > 1:
        stages.append([("slab", core * z, y)])
    return stages


def stage_partners(digits, slab, sub):
    total = 1
    for _, _, size in digits:
        total *= size
    partners = []
    for offset in range(1, total):
        rest, at = offset, {"slab": slab, "sub": sub}
        for axis, stride, size in digits:
            step, rest = rest % size, rest // size
            digit = (at[axis] // stride) % size
            at[axis] = at[axis] + ((digit + step) % size - digit) * stride
        partners.append((at["slab"], at["sub"]))
    return partners


def total_of(terms):
    terms = list(terms)
    while len(terms) > 1:
        terms = [sum(terms[i : i + 2][1:], terms[i]) for i in range(0, len(terms), 2)]
    return terms[0]


def kernel(
    n_slab,
    n_sub,
    stages,
    m_any,
    ss_any,
    cs_any,
    sg_any,
    cg_any,
    gr_any,
    len_any,
    x_ref,
    r_ref,
    len_ref,
    m_in,
    ss,
    cs,
    sg,
    cg,
    gr,
    field,
    r0,
    z0,
    q0,
    d0,
    ssb,
    csb,
    fac,
    ts,
    us,
    tc,
    uc,
    prod,
    flip,
    coef_send,
    coef_span,
    coef_chord,
    row_first,
    row_last,
    from_ahead,
    from_behind,
    col_own,
    col_ahead,
    col_behind,
    w_ahead,
    w_behind,
    w_col,
    t_send,
    u_send,
    u_ahead,
    t_behind,
    tu_send,
    tu_ahead,
    tu_behind,
    *rest,
):
    parts = rest[: len(stages)]
    in_sem, send_sem, recv_sem = rest[len(stages) :]
    slab, sub = lax.axis_index("slab"), lax.axis_index("sub")
    ahead = (lax.rem(slab + 1, n_slab), sub)
    behind = (lax.rem(slab + n_slab - 1, n_slab), sub)
    right = (slab, lax.rem(sub + 1, n_sub))
    left = (slab, lax.rem(sub + n_sub - 1, n_sub))
    partners = [stage_partners(digits, slab, sub) for digits in stages]

    loads = []
    for k, (source, target) in enumerate(
        ((m_any, m_in), (ss_any, ss), (cs_any, cs), (sg_any, sg), (cg_any, cg), (gr_any, gr), (len_any, len_ref))
    ):
        copy = pltpu.make_async_copy(source, target, in_sem.at[k])
        copy.start()
        loads.append(copy)

    barrier = pltpu.get_barrier_semaphore()
    greeted = [ahead, behind, right, left] + [p for group in partners for p in group]
    for device in greeted:
        pl.semaphore_signal(barrier, inc=1, device_id=device, device_id_type=MESH)

    row = lax.broadcasted_iota(jnp.int32, (R, C), 0)
    lane = lax.broadcasted_iota(jnp.int32, (R, C), 1)
    pair = lax.shift_right_logical(lane, 1)
    even = lane - 2 * pair == 0

    def tile(k):
        return pl.ds(pl.multiple_of(k * R, R), R)

    def wide(value):
        return jnp.broadcast_to(value, (R, C))

    sent = []
    count = [0]

    def send(source, target, device):
        k = count[0]
        count[0] += 1
        copy = pltpu.make_async_remote_copy(
            src_ref=source,
            dst_ref=target,
            send_sem=send_sem.at[k],
            recv_sem=recv_sem.at[k],
            device_id=device,
            device_id_type=MESH,
        )
        copy.start()
        sent.append(copy)
        return copy

    loads[0].wait()

    def pack(i, packs):
        packs = list(packs)
        for u in range(UNROLL):
            j = i * UNROLL + u
            for c in range(D):
                value = m_in[j, c].astype(jnp.float32)
                field[tile(j * D + c), :] = value
                half = 32 * (c % 2)
                turned = pltpu.roll(value, 2 * (j + half) + 1, 1)
                packs[c // 2] = jnp.where(pair == j + half, turned, packs[c // 2])
        return tuple(packs)

    zero = jnp.zeros((R, C), jnp.float32)
    packs = lax.fori_loop(0, M // UNROLL, pack, (zero,) * 3)
    for v in range(3):
        col_own[pl.ds(v * R, R), :] = packs[v]
    for g in range(M // 8):
        for c in range(D):
            at = pl.ds((g * D + c) * 8, 8)
            row_first[at, :] = field[pl.ds((g * 8 * D + c) * R, 8, stride=D * R), :]
            row_last[at, :] = field[pl.ds((g * 8 * D + c) * R + R - 1, 8, stride=D * R), :]

    for copy in loads[1:]:
        copy.wait()
    span_coef, chord_coef = zero, zero
    for c in range(D + 1):
        mine = ss[c] if c < D else sg[...]
        span_coef = jnp.where(row == c, wide(mine[R - 1 :, :]), span_coef)
        mine = cs[c] if c < D else cg[...]
        chord_coef = jnp.where(lane == c, wide(mine[:, C - 1 :]), chord_coef)
    coef_send[0] = span_coef
    coef_send[1] = chord_coef

    pl.semaphore_wait(barrier, len(greeted))
    got_coef = [
        send(coef_send.at[0], coef_span, ahead),
        send(coef_send.at[1], coef_chord, right),
    ]
    got_cols = [send(col_own, col_behind, right), send(col_own, col_ahead, left)]
    got_rows = []
    for g in range(M // 8):
        at = pl.ds(g * 8 * D, 8 * D)
        got_rows.append(
            [
                send(row_last.at[at], from_behind.at[at], ahead),
                send(row_first.at[at], from_ahead.at[at], behind),
            ]
        )

    n_stations = n_slab * R
    first = slab * R
    length = jnp.zeros((R, C), jnp.int32)
    length_next = jnp.zeros((R, C), jnp.int32)
    length_prev = jnp.zeros((R, C), jnp.int32)
    for k in range(-1, R + 1):
        here = len_ref[jnp.clip(first + k, 0, n_stations - 1)]
        if 0 <= k < R:
            length = jnp.where(row == k, here, length)
        if k >= 1:
            length_next = jnp.where(row == k - 1, here, length_next)
        if k < R - 1:
            length_prev = jnp.where(row == k + 1, here, length_prev)
    column = lane + sub * C
    station = row + first
    one = jnp.ones((R, C), jnp.float32)
    span_live = jnp.where(
        (column < length) & (column < length_next) & (station < n_stations - 1), one, zero
    )
    span_live_b = jnp.where(
        (column < length) & (column < length_prev) & (station > 0), one, zero
    )
    chord_live = jnp.where(column + 1 < length, one, zero)
    chord_live_b = jnp.where((column < length) & (column > 0), one, zero)
    span_geo = sg[...] * span_live
    chord_geo = cg[...] * chord_live

    for copy in got_coef:
        copy.wait_recv()
    chord_ghost = coef_chord[...]
    for c in range(D):
        mine = ss[c]
        back = jnp.where(row == 0, wide(coef_span[pl.ds(c, 1), :]), pltpu.roll(mine, 1, 0))
        ssb[c] = back * span_live_b
        ss[c] = mine * span_live
        mine = cs[c]
        back = jnp.where(lane == 0, wide(chord_ghost[:, c : c + 1]), pltpu.roll(mine, 1, 1))
        csb[c] = back * chord_live_b
        cs[c] = mine * chord_live
    a_s = [ss[c] for c in range(D)]
    a_c = [cs[c] for c in range(D)]
    b_s = [ssb[c] for c in range(D)]
    b_c = [csb[c] for c in range(D)]
    low = [[None] * D for _ in range(D)]
    raw = [[None] * D for _ in range(D)]
    k = 0
    for j in range(D):
        for i in range(j, D):
            entry = (a_s[i] * a_s[j] + b_s[i] * b_s[j]) + (a_c[i] * a_c[j] + b_c[i] * b_c[j])
            if i == j:
                entry = entry + gr[i]
            for n in range(j):
                entry = entry - raw[i][n] * low[j][n]
            raw[i][j] = entry
        inverse = 1.0 / raw[j][j]
        fac[15 + j] = inverse
        for i in range(j + 1, D):
            low[i][j] = raw[i][j] * inverse
            fac[k] = low[i][j]
            k += 1

    def factors():
        low = {}
        k = 0
        for j in range(D):
            for i in range(j + 1, D):
                low[i, j] = fac[k]
                k += 1
        return low, [fac[15 + j] for j in range(D)]

    def solve(vector):
        low, inverse = factors()
        forward = []
        for i in range(D):
            running = vector[i]
            for j in range(i):
                running = running - low[i, j] * forward[j]
            forward.append(running)
        backward = [None] * D
        for i in reversed(range(D)):
            running = forward[i] * inverse[i]
            for j in range(i + 1, D):
                running = running - low[j, i] * backward[j]
            backward[i] = running
        return backward

    def dots(j, vector, packed):
        t_s = total_of(ss[c] * vector[c] for c in range(D))
        u_s = total_of(ssb[c] * vector[c] for c in range(D))
        t_c = total_of(cs[c] * vector[c] for c in range(D))
        u_c = total_of(csb[c] * vector[c] for c in range(D))
        ts[tile(j), :] = t_s
        us[tile(j), :] = u_s
        tc[tile(j), :] = t_c
        uc[tile(j), :] = u_c
        turned = pltpu.roll(jnp.where(lane == 0, u_c, t_c), 2 * j + 1, 1)
        return jnp.where(pair == j, turned, packed)

    def send_dots(turn, g, packed):
        at = pl.ds(turn * M + g * GM, GM)
        for b in range(GM // 8):
            from_mode = g * GM + b * 8
            to = pl.ds(turn * M + from_mode, 8)
            t_send[to, :] = ts[pl.ds(from_mode * R + R - 1, 8, stride=R), :]
            u_send[to, :] = us[pl.ds(from_mode * R, 8, stride=R), :]
        tu_send[turn, g] = packed
        return [
            send(t_send.at[at], t_behind.at[at], ahead),
            send(u_send.at[at], u_ahead.at[at], behind),
            send(tu_send.at[turn, g], tu_behind.at[turn, g], right),
            send(tu_send.at[turn, g], tu_ahead.at[turn, g], left),
        ]

    def edges_of(turn, g):
        return jnp.where(
            even,
            pltpu.roll(tu_ahead[turn, g], C - 1, 1),
            pltpu.roll(tu_behind[turn, g], 1, 1),
        )

    def operate(turn, j, vector, edge):
        t_s, u_s, t_c, u_c = ts[tile(j), :], us[tile(j), :], tc[tile(j), :], uc[tile(j), :]
        at = pl.ds(turn * M + j, 1)
        edge = pltpu.roll(edge, C - 1 - 2 * j, 1)
        u_s_next = jnp.where(row == R - 1, wide(u_ahead[at, :]), pltpu.roll(u_s, R - 1, 0))
        t_s_prev = jnp.where(row == 0, wide(t_behind[at, :]), pltpu.roll(t_s, 1, 0))
        u_c_next = jnp.where(lane == C - 1, edge, pltpu.roll(u_c, C - 1, 1))
        t_c_prev = jnp.where(lane == 0, edge, pltpu.roll(t_c, 1, 1))
        e_s, e_sb = u_s_next - t_s, u_s - t_s_prev
        e_c, e_cb = u_c_next - t_c, u_c - t_c_prev
        return [
            (gr[c] * vector[c] + (ssb[c] * e_sb - ss[c] * e_s)) + (csb[c] * e_cb - cs[c] * e_c)
            for c in range(D)
        ]

    def of_mode(ref, j):
        return [ref[tile(j * D + c), :] for c in range(D)]

    def keep(ref, j, vector):
        for c in range(D):
            ref[tile(j * D + c), :] = vector[c]

    def over_group(g, step, carry):
        def some(i, carry):
            for u in range(UNROLL):
                carry = step(g * GM + i * UNROLL + u, carry)
            return carry

        return lax.fori_loop(0, GM // UNROLL, some, carry)

    for copy in got_cols:
        copy.wait_recv()
    square = None
    for v in range(3):
        at = pl.ds(v * R, R)
        across = jnp.where(
            even, pltpu.roll(col_ahead[at, :], C - 1, 1), pltpu.roll(col_behind[at, :], 1, 1)
        )
        jump = across - col_own[at, :]
        square = jump * jump if square is None else square + jump * jump
    square = square + pltpu.roll(square, C // 2, 1)
    geo_b = chord_ghost[:, D : D + 1] * chord_live_b[:, :1]
    w_col[...] = square * jnp.where(even, wide(chord_geo[:, C - 1 :]), wide(geo_b))
    sg[...] = span_geo
    cg[...] = chord_geo
    geo_ahead = jnp.broadcast_to(span_geo[R - 1 :, :], (8, C))
    geo_behind = jnp.broadcast_to(coef_span[pl.ds(D, 1), :] * span_live_b[:1, :], (8, C))

    def load_step(j, packed):
        modes = of_mode(field, j)
        edge = pltpu.roll(w_col[...], C - 1 - 2 * j, 1)
        jumps = [pltpu.roll(value, R - 1, 0) - value for value in modes]
        w_s = total_of(jump * jump for jump in jumps) * sg[...]
        w_s = jnp.where(row == R - 1, wide(w_ahead[pl.ds(j, 1), :]), w_s)
        jumps = [pltpu.roll(value, C - 1, 1) - value for value in modes]
        w_c = total_of(jump * jump for jump in jumps) * cg[...]
        w_c = jnp.where(lane == C - 1, edge, w_c)
        w_sb = jnp.where(row == 0, wide(w_behind[pl.ds(j, 1), :]), pltpu.roll(w_s, 1, 0))
        w_cb = jnp.where(lane == 0, edge, pltpu.roll(w_c, 1, 1))
        load = [
            (ssb[c] * w_sb - ss[c] * w_s) + (csb[c] * w_cb - cs[c] * w_c) for c in range(D)
        ]
        first_z = solve(load)
        keep(r0, j, load)
        keep(z0, j, first_z)
        return dots(j, first_z, packed)

    got_first = []
    for g in range(GROUPS):
        for b in range(GM // 8):
            block = g * (GM // 8) + b
            for copy in got_rows[block]:
                copy.wait_recv()
            to_ahead, to_behind = [], []
            for c in range(D):
                at = pl.ds((block * D + c) * 8, 8)
                jump = from_ahead[at, :] - row_last[at, :]
                to_ahead.append(jump * jump)
                jump = row_first[at, :] - from_behind[at, :]
                to_behind.append(jump * jump)
            w_ahead[pl.ds(block * 8, 8), :] = total_of(to_ahead) * geo_ahead
            w_behind[pl.ds(block * 8, 8), :] = total_of(to_behind) * geo_behind
        got_first.append(send_dots(0, g, over_group(g, load_step, zero)))

    def first_step(edge, j, packed):
        z = of_mode(z0, j)
        image = operate(0, j, z, edge)
        left_over = [a - b for a, b in zip(of_mode(r0, j), image)]
        second = solve(left_over)
        keep(q0, j, image)
        keep(d0, j, second)
        prod[tile(j), :] = total_of(a * b for a, b in zip(z, image))
        prod[tile(M + j), :] = total_of(a * b for a, b in zip(z, left_over))
        prod[tile(2 * M + j), :] = total_of(a * b for a, b in zip(second, left_over))
        return dots(j, second, packed)

    got_second = []
    for g in range(GROUPS):
        for copy in got_first[g]:
            copy.wait_recv()
        edge = edges_of(0, g)
        packed = over_group(g, functools.partial(first_step, edge), zero)
        got_second.append(send_dots(1, g, packed))

    def fold(k):
        rows = [prod[pl.ds(k * 8 * R + n, 8, stride=R), :] for n in range(R)]
        flip[pl.ds(k * 8, 8), :] = total_of(rows)

    for k in range(3 * M // 8):
        fold(k)

    def second_step(edge, j, carry):
        second = of_mode(d0, j)
        image = operate(1, j, second, edge)
        keep(field, j, image)
        prod[tile(3 * M + j), :] = total_of(a * b for a, b in zip(second, image))
        return carry

    for g in range(GROUPS):
        for copy in got_second[g]:
            copy.wait_recv()
        over_group(g, functools.partial(second_step, edges_of(1, g)), 0)
    for k in range(3 * M // 8, 4 * M // 8):
        fold(k)

    own = jnp.sum(jnp.transpose(flip[...]), axis=0, keepdims=True)
    for part, group in zip(parts, partners):
        members = len(group) + 1
        part[pl.ds(0, 1), :] = own
        copies = [
            send(part.at[pl.ds(0, 1)], part.at[pl.ds(n + 1, 1)], device)
            for n, device in enumerate(group)
        ]
        for copy in copies:
            copy.wait_recv()
        own = jnp.sum(part[pl.ds(0, members), :], axis=0, keepdims=True)

    zq = wide(own)
    zs = pltpu.roll(zq, C - M, 1)
    ds = pltpu.roll(zq, C - 2 * M, 1)
    dv = pltpu.roll(zq, C - 3 * M, 1)
    dq = zs - ds
    ratio = dq / zq
    second_part = (ds - dq * (zs / zq)) / (dv - ratio * dq)
    excess = (zs - dq * second_part) / zq

    def last_step(j, carry):
        turned = lax.rem(C - j, C)
        over = wide(pltpu.roll(excess, turned, 1)[:, :1])
        other = wide(pltpu.roll(second_part, turned, 1)[:, :1])
        main = 1.0 + over
        for c in range(D):
            at = tile(j * D + c)
            image = q0[at, :]
            x_ref[at, :] = main * z0[at, :] + other * d0[at, :]
            r_ref[at, :] = ((r0[at, :] - image) - over * image) - other * field[at, :]
        return carry

    for g in range(GROUPS):
        over_group(g, last_step, 0)
    for copy in sent:
        copy.wait_send()


def body(n_slab, n_sub, mode_shapes, span_stiff, chord_stiff, span_geo, chord_geo, ground, chord_len):
    stages = digit_stages(n_slab, n_sub)
    f32 = jnp.float32
    members = []
    for digits in stages:
        total = 1
        for _, _, size in digits:
            total *= size
        members.append(total)
    n_sends = 4 + 2 * (M // 8) + 8 * GROUPS + sum(members) - len(members)

    def big():
        return pltpu.VMEM((M * D * R, C), f32)

    rows = M * D
    scratch = [
        pltpu.SMEM(chord_len.shape, jnp.int32),
        pltpu.VMEM((M, D, R, C), jnp.bfloat16),
        pltpu.VMEM((D, R, C), f32),
        pltpu.VMEM((D, R, C), f32),
        pltpu.VMEM((R, C), f32),
        pltpu.VMEM((R, C), f32),
        pltpu.VMEM((D, R, C), f32),
        big(),
        big(),
        big(),
        big(),
        big(),
        pltpu.VMEM((D, R, C), f32),
        pltpu.VMEM((D, R, C), f32),
        pltpu.VMEM((21, R, C), f32),
        pltpu.VMEM((M * R, C), f32),
        pltpu.VMEM((M * R, C), f32),
        pltpu.VMEM((M * R, C), f32),
        pltpu.VMEM((M * R, C), f32),
        pltpu.VMEM((4 * M * R, C), f32),
        pltpu.VMEM((4 * M, C), f32),
        pltpu.VMEM((2, R, C), f32),
        pltpu.VMEM((R, C), f32),
        pltpu.VMEM((R, C), f32),
        pltpu.VMEM((rows, C), f32),
        pltpu.VMEM((rows, C), f32),
        pltpu.VMEM((rows, C), f32),
        pltpu.VMEM((rows, C), f32),
        pltpu.VMEM((3 * R, C), f32),
        pltpu.VMEM((3 * R, C), f32),
        pltpu.VMEM((3 * R, C), f32),
        pltpu.VMEM((M, C), f32),
        pltpu.VMEM((M, C), f32),
        pltpu.VMEM((R, C), f32),
        pltpu.VMEM((2 * M, C), f32),
        pltpu.VMEM((2 * M, C), f32),
        pltpu.VMEM((2 * M, C), f32),
        pltpu.VMEM((2 * M, C), f32),
        pltpu.VMEM((2, GROUPS, R, C), f32),
        pltpu.VMEM((2, GROUPS, R, C), f32),
        pltpu.VMEM((2, GROUPS, R, C), f32),
    ]
    scratch += [pltpu.VMEM((max(8, n), C), f32) for n in members]
    scratch += [
        pltpu.SemaphoreType.DMA((7,)),
        pltpu.SemaphoreType.DMA((n_sends,)),
        pltpu.SemaphoreType.DMA((n_sends,)),
    ]
    in_hbm = pl.BlockSpec(memory_space=pltpu.HBM)
    shape = jax.ShapeDtypeStruct((M * D * R, C), f32)
    adjoint, residual = pl.pallas_call(
        functools.partial(kernel, n_slab, n_sub, stages),
        out_shape=(shape, shape),
        in_specs=[in_hbm] * 7,
        out_specs=(pl.BlockSpec(memory_space=pltpu.VMEM),) * 2,
        scratch_shapes=scratch,
        compiler_params=pltpu.CompilerParams(
            collective_id=0, has_side_effects=True, vmem_limit_bytes=24 << 20
        ),
    )(mode_shapes, span_stiff, chord_stiff, span_geo, chord_geo, ground, chord_len)
    full = (M, D, R, C)
    return adjoint.reshape(full), residual.reshape(full)


def solution(mesh):
    sizes = (mesh.shape["slab"], mesh.shape["sub"])
    return jax.shard_map(
        functools.partial(body, *sizes),
        mesh=mesh,
        in_specs=(
            P(None, None, "slab", "sub"),
            P(None, "slab", "sub"),
            P(None, "slab", "sub"),
            P("slab", "sub"),
            P("slab", "sub"),
            P(None, "slab", "sub"),
            P(),
        ),
        out_specs=(P(None, None, "slab", "sub"), P(None, None, "slab", "sub")),
        check_vma=False,
    )
```

time: 415 us -> 56.3 us (0.14)
  blocking collectives: 312 us -> 0 us
  Pallas kernels: 0 us -> 47.9 us
  starting transfers between devices: 41.7 us -> 0 us
  local copies, waits for them, and re-layouts: 31.7 us -> 7.02 us
  other arithmetic: 21.5 us -> 0 us
  waiting for transfers between devices: 4.56 us -> 0 us
    psum x3 -> x0, blocking collectives: 312 us -> none  [the longest x2 212 us: inner_rz(): return lax.psum(jnp.sum(first * second, axis=(1, 2, 3)), ('slab', 'sub'))]
    pallas_call x0 -> x1, Pallas kernels: none -> 47.9 us  [body(): pl.pallas_call(functools.partial(kernel, n_slab, n_sub, stages), out_shap...]
    ppermute x14 -> x0, starting transfers between devices: 41.7 us -> none  [from_behind(): lax.ppermute(value, axis, [(source, source + steps) for source in range(i...]
    slice x30 -> x0, local copies, waits for them, and re-layouts: 15.4 us -> none  [the longest x6 6.48 us: forces_behind(): from_chord = from_behind(chord_forces[:, :, :, -1:], 'sub', 1)]
    reduce_sum x6 -> x0, other arithmetic: 9.34 us -> none  [the longest x2 5.36 us: inner_pq(): return lax.psum(jnp.sum(first * second, axis=(1, 2, 3)), ('slab', 'sub'))]
    ppermute x6 -> x0, local copies, waits for them, and re-layouts: 5.55 us -> none  [from_behind(): lax.ppermute(value, axis, [(source, source + steps) for source in range(i...]
    ppermute x14 -> x0, waiting for transfers between devices: 4.56 us -> none  [from_behind(): lax.ppermute(value, axis, [(source, source + steps) for source in range(i...]
    unnamed x64 -> x16, local copies, waits for them, and re-layouts: 10.6 us -> 7.02 us
  transfers between devices with their start and end apart: 14 -> 0, of which waited for: 4 -> 0; matrix products, arithmetic and copies ran while one was open for 6% -> 0% of each run, Pallas kernels for 0% -> 0%
where the time goes in v1:
time: 56.3 us; the launch traced here: 55.6 us
  Pallas kernels  47.9 us (85%)
  local copies, waits for them, and re-layouts  7.02 us (12%)
  between operations  0.66 us (1%)
    pallas_call x1, Pallas kernels, body(): pl.pallas_call(functools.partial(kernel, n_slab, n_sub, stages), out_shap...  47.9 us
    unnamed x16, local copies, waits for them, and re-layouts  7.02 us

profile of v1, /device:TPU:1, one launch (start us, length us, event | category | flops | bytes accessed | tf_op | source)
XLA Modules:
  0.0 55.6 jit_solution(9217907176616954531)
XLA Ops:
  0.6 0.0 copy-start
  0.6 1.0 %copy-done = bf16[32,6,8,128]{3,2,1,0:T(8,128)(2,1)S(1)} copy-done((bf16[32,6,8,128]{3,2,1,0:T(8,128)(2,1)S(1)}, bf16[32,6,8,128]{3,2,1,0:T(8,128)(2,1)}, u32[]{:S(2)}) %copy-start) | copy-done | bytes 393240
  1.6 0.0 copy-start.1
  1.6 0.7 %copy-done.1 = f32[6,8,128]{2,1,0:T(8,128)S(1)} copy-done((f32[6,8,128]{2,1,0:T(8,128)S(1)}, f32[6,8,128]{2,1,0:T(8,128)}, u32[]{:S(2)}) %copy-start.1) | copy-done | bytes 24600
  2.4 0.0 copy-start.2
  2.4 0.7 %copy-done.2 = f32[6,8,128]{2,1,0:T(8,128)S(1)} copy-done((f32[6,8,128]{2,1,0:T(8,128)S(1)}, f32[6,8,128]{2,1,0:T(8,128)}, u32[]{:S(2)}) %copy-start.2) | copy-done | bytes 24600
  3.1 0.0 copy-start.3
  3.1 0.7 %copy-done.3 = f32[6,8,128]{2,1,0:T(8,128)S(1)} copy-done((f32[6,8,128]{2,1,0:T(8,128)S(1)}, f32[6,8,128]{2,1,0:T(8,128)}, u32[]{:S(2)}) %copy-start.3) | copy-done | bytes 24600
  3.8 0.0 copy-start.4
  3.8 0.7 %copy-done.4 = f32[8,128]{1,0:T(8,128)S(1)} copy-done((f32[8,128]{1,0:T(8,128)S(1)}, f32[8,128]{1,0:T(8,128)}, u32[]{:S(2)}) %copy-start.4) | copy-done | bytes 4120
  4.5 0.0 copy-start.5
  4.5 0.7 %copy-done.5 = f32[8,128]{1,0:T(8,128)S(1)} copy-done((f32[8,128]{1,0:T(8,128)S(1)}, f32[8,128]{1,0:T(8,128)}, u32[]{:S(2)}) %copy-start.5) | copy-done | bytes 4120
  5.2 0.0 copy-start.6
  5.2 0.7 %copy-done.6 = s32[1024]{0:T(1024)S(1)} copy-done((s32[1024]{0:T(1024)S(1)}, s32[1024]{0:T(1024)}, u32[]{:S(2)}) %copy-start.6) | copy-done | bytes 4120
  5.9 47.9 %shard_map.86 = (f32[1536,128]{1,0:T(8,128)S(1)}, f32[1536,128]{1,0:T(8,128)S(1)}) custom-call(bf16[32,6,8,128]{3,2,1,0:T(8,128)(2,1)S(1)} %copy-done, f32[6,8,128]{2,1,0:T(8,128)S(1)} %copy-done.1, f32[6,8,128]{2,1,0:T(8,128)S(1)} %copy-done.2, f32[8,128]{1,0:T(8,128)S(1)} %copy-done.4, f32[8,128]{1,0:T(8,128)S(1)} %copy-done.5, ...), custom_call_target="tpu_custom_call" | custom-call | tf_op jit(solution)/shard_map/pallas_call | solution.py:561
  53.8 0.9 %copy.11 = f32[32,6,8,128]{3,2,1,0:T(8,128)} copy(f32[32,6,8,128]{3,2,1,0:T(8,128)S(1)} %bitcast.3) | data formatting | bytes 1572864
  54.7 0.9 %copy.12 = f32[32,6,8,128]{3,2,1,0:T(8,128)} copy(f32[32,6,8,128]{3,2,1,0:T(8,128)S(1)} %bitcast.2) | data formatting | bytes 1572864
Async XLA Ops:
  0.6 1.0 %copy-start = (bf16[32,6,8,128]{3,2,1,0:T(8,128)(2,1)S(1)}, bf16[32,6,8,128]{3,2,1,0:T(8,128)(2,1)}, u32[]{:S(2)}) copy-start(bf16[32,6,8,128]{3,2,1,0:T(8,128)(2,1)} %m_any.1) | copy-start | bytes 1179652
  1.6 0.7 %copy-start.1 = (f32[6,8,128]{2,1,0:T(8,128)S(1)}, f32[6,8,128]{2,1,0:T(8,128)}, u32[]{:S(2)}) copy-start(f32[6,8,128]{2,1,0:T(8,128)} %ss_any.1) | copy-start | bytes 73732
  2.4 0.7 %copy-start.2 = (f32[6,8,128]{2,1,0:T(8,128)S(1)}, f32[6,8,128]{2,1,0:T(8,128)}, u32[]{:S(2)}) copy-start(f32[6,8,128]{2,1,0:T(8,128)} %cs_any.1) | copy-start | bytes 73732
  3.1 0.7 %copy-start.3 = (f32[6,8,128]{2,1,0:T(8,128)S(1)}, f32[6,8,128]{2,1,0:T(8,128)}, u32[]{:S(2)}) copy-start(f32[6,8,128]{2,1,0:T(8,128)} %gr_any.1) | copy-start | bytes 73732
  3.8 0.7 %copy-start.4 = (f32[8,128]{1,0:T(8,128)S(1)}, f32[8,128]{1,0:T(8,128)}, u32[]{:S(2)}) copy-start(f32[8,128]{1,0:T(8,128)} %sg_any.1) | copy-start | bytes 12292
  4.5 0.7 %copy-start.5 = (f32[8,128]{1,0:T(8,128)S(1)}, f32[8,128]{1,0:T(8,128)}, u32[]{:S(2)}) copy-start(f32[8,128]{1,0:T(8,128)} %cg_any.1) | copy-start | bytes 12292
  5.2 0.7 %copy-start.6 = (s32[1024]{0:T(1024)S(1)}, s32[1024]{0:T(1024)}, u32[]{:S(2)}) copy-start(s32[1024]{0:T(1024)} %len_any.1) | copy-start | bytes 12292

commit v2 on v1

--- a/solution.py
+++ b/solution.py
@@ -13,19 +13,17 @@
 M = 32
 GROUPS = 4
 GM = M // GROUPS
-UNROLL = 2
+UNROLL = 4
 
 
 def digit_stages(n_slab, n_sub):
     core = 2
     z = 16 if n_slab % 32 == 0 else 1
     y = n_slab // (core * z)
-    stages = [[("slab", 1, core), ("sub", 1, n_sub)]]
-    if z > 1:
-        stages.append([("slab", core, z)])
+    near = [("slab", 1, core), ("sub", 1, n_sub)]
     if y > 1:
-        stages.append([("slab", core * z, y)])
-    return stages
+        near.append(("slab", core * z, y))
+    return [near, [("slab", core, z)]] if z > 1 else [near]
 
 
 def stage_partners(digits, slab, sub):
@@ -48,6 +46,11 @@
     while len(terms) > 1:
         terms = [sum(terms[i : i + 2][1:], terms[i]) for i in range(0, len(terms), 2)]
     return terms[0]
+
+
+def place(i, j):
+    i, j = min(i, j), max(i, j)
+    return i * D - i * (i - 1) // 2 + j - i
 
 
 def kernel(
@@ -139,6 +142,21 @@
     def wide(value):
         return jnp.broadcast_to(value, (R, C))
 
+    def of_mode(ref, j):
+        return [ref[tile(j * D + c), :] for c in range(D)]
+
+    def keep(ref, j, vector):
+        for c in range(D):
+            ref[tile(j * D + c), :] = vector[c]
+
+    def over_group(g, step, carry):
+        def some(i, carry):
+            for u in range(UNROLL):
+                carry = step(g * GM + i * UNROLL + u, carry)
+            return carry
+
+        return lax.fori_loop(0, GM // UNROLL, some, carry)
+
     sent = []
     count = [0]
 
@@ -235,6 +253,20 @@
     span_geo = sg[...] * span_live
     chord_geo = cg[...] * chord_live
 
+    sg[...] = span_geo
+    cg[...] = chord_geo
+
+    def weigh(j, carry):
+        modes = of_mode(field, j)
+        jumps = [pltpu.roll(value, R - 1, 0) - value for value in modes]
+        ts[tile(j), :] = total_of(jump * jump for jump in jumps) * sg[...]
+        jumps = [pltpu.roll(value, C - 1, 1) - value for value in modes]
+        tc[tile(j), :] = total_of(jump * jump for jump in jumps) * cg[...]
+        return carry
+
+    for g in range(GROUPS):
+        over_group(g, weigh, 0)
+
     for copy in got_coef:
         copy.wait_recv()
     chord_ghost = coef_chord[...]
@@ -253,7 +285,7 @@
     b_c = [csb[c] for c in range(D)]
     low = [[None] * D for _ in range(D)]
     raw = [[None] * D for _ in range(D)]
-    k = 0
+    inverse = []
     for j in range(D):
         for i in range(j, D):
             entry = (a_s[i] * a_s[j] + b_s[i] * b_s[j]) + (a_c[i] * a_c[j] + b_c[i] * b_c[j])
@@ -262,37 +294,29 @@
             for n in range(j):
                 entry = entry - raw[i][n] * low[j][n]
             raw[i][j] = entry
-        inverse = 1.0 / raw[j][j]
-        fac[15 + j] = inverse
+        inverse.append(1.0 / raw[j][j])
         for i in range(j + 1, D):
-            low[i][j] = raw[i][j] * inverse
-            fac[k] = low[i][j]
-            k += 1
-
-    def factors():
-        low = {}
-        k = 0
-        for j in range(D):
-            for i in range(j + 1, D):
-                low[i, j] = fac[k]
-                k += 1
-        return low, [fac[15 + j] for j in range(D)]
+            low[i][j] = raw[i][j] * inverse[j]
+    unit = [[None] * D for _ in range(D)]
+    for j in range(D):
+        for i in range(j + 1, D):
+            entry = low[i][j]
+            for n in range(j + 1, i):
+                entry = entry + low[i][n] * unit[n][j]
+            unit[i][j] = -entry
+    scaled = [[None] * D for _ in range(D)]
+    for k in range(D):
+        for i in range(k):
+            scaled[k][i] = unit[k][i] * inverse[k]
+        scaled[k][k] = inverse[k]
+    for i in range(D):
+        for j in range(i, D):
+            terms = [scaled[j][i] if i < j else inverse[j]]
+            terms += [scaled[k][i] * unit[k][j] for k in range(j + 1, D)]
+            fac[place(i, j)] = total_of(terms)
 
     def solve(vector):
-        low, inverse = factors()
-        forward = []
-        for i in range(D):
-            running = vector[i]
-            for j in range(i):
-                running = running - low[i, j] * forward[j]
-            forward.append(running)
-        backward = [None] * D
-        for i in reversed(range(D)):
-            running = forward[i] * inverse[i]
-            for j in range(i + 1, D):
-                running = running - low[j, i] * backward[j]
-            backward[i] = running
-        return backward
+        return [total_of(fac[place(i, j)] * vector[j] for j in range(D)) for i in range(D)]
 
     def dots(j, vector, packed):
         t_s = total_of(ss[c] * vector[c] for c in range(D))
@@ -343,21 +367,6 @@
             for c in range(D)
         ]
 
-    def of_mode(ref, j):
-        return [ref[tile(j * D + c), :] for c in range(D)]
-
-    def keep(ref, j, vector):
-        for c in range(D):
-            ref[tile(j * D + c), :] = vector[c]
-
-    def over_group(g, step, carry):
-        def some(i, carry):
-            for u in range(UNROLL):
-                carry = step(g * GM + i * UNROLL + u, carry)
-            return carry
-
-        return lax.fori_loop(0, GM // UNROLL, some, carry)
-
     for copy in got_cols:
         copy.wait_recv()
     square = None
@@ -371,20 +380,13 @@
     square = square + pltpu.roll(square, C // 2, 1)
     geo_b = chord_ghost[:, D : D + 1] * chord_live_b[:, :1]
     w_col[...] = square * jnp.where(even, wide(chord_geo[:, C - 1 :]), wide(geo_b))
-    sg[...] = span_geo
-    cg[...] = chord_geo
     geo_ahead = jnp.broadcast_to(span_geo[R - 1 :, :], (8, C))
     geo_behind = jnp.broadcast_to(coef_span[pl.ds(D, 1), :] * span_live_b[:1, :], (8, C))
 
     def load_step(j, packed):
-        modes = of_mode(field, j)
         edge = pltpu.roll(w_col[...], C - 1 - 2 * j, 1)
-        jumps = [pltpu.roll(value, R - 1, 0) - value for value in modes]
-        w_s = total_of(jump * jump for jump in jumps) * sg[...]
-        w_s = jnp.where(row == R - 1, wide(w_ahead[pl.ds(j, 1), :]), w_s)
-        jumps = [pltpu.roll(value, C - 1, 1) - value for value in modes]
-        w_c = total_of(jump * jump for jump in jumps) * cg[...]
-        w_c = jnp.where(lane == C - 1, edge, w_c)
+        w_s = jnp.where(row == R - 1, wide(w_ahead[pl.ds(j, 1), :]), ts[tile(j), :])
+        w_c = jnp.where(lane == C - 1, edge, tc[tile(j), :])
         w_sb = jnp.where(row == 0, wide(w_behind[pl.ds(j, 1), :]), pltpu.roll(w_s, 1, 0))
         w_cb = jnp.where(lane == 0, edge, pltpu.roll(w_c, 1, 1))
         load = [
@@ -556,6 +558,12 @@
         pltpu.SemaphoreType.DMA((n_sends,)),
         pltpu.SemaphoreType.DMA((n_sends,)),
     ]
+    operands = [
+        pltpu.with_memory_space_constraint(value, pltpu.HBM)
+        for value in (
+            mode_shapes, span_stiff, chord_stiff, span_geo, chord_geo, ground, chord_len
+        )
+    ]
     in_hbm = pl.BlockSpec(memory_space=pltpu.HBM)
     shape = jax.ShapeDtypeStruct((M * D * R, C), f32)
     adjoint, residual = pl.pallas_call(
@@ -567,7 +575,7 @@
         compiler_params=pltpu.CompilerParams(
             collective_id=0, has_side_effects=True, vmem_limit_bytes=24 << 20
         ),
-    )(mode_shapes, span_stiff, chord_stiff, span_geo, chord_geo, ground, chord_len)
+    )(*operands)
     full = (M, D, R, C)
     return adjoint.reshape(full), residual.reshape(full)
 

time: 56.3 us -> 46.2 us (0.82); the launches traced: 55.6 us -> 46.1 us
  local copies, waits for them, and re-layouts: 7.02 us -> 1.76 us
  Pallas kernels: 47.9 us -> 43.7 us
    unnamed x16 -> x2, local copies, waits for them, and re-layouts: 7.02 us -> 1.76 us
    pallas_call x1, Pallas kernels: 47.9 us -> 43.7 us  [body(): pl.pallas_call(functools.partial(kernel, n_slab, n_sub, stages), out_shap...]
where the time goes in v2:
time: 46.2 us; the launch traced here: 46.1 us
  Pallas kernels  43.7 us (95%)
  local copies, waits for them, and re-layouts  1.76 us (4%)
  between operations  0.64 us (1%)
    pallas_call x1, Pallas kernels, body(): pl.pallas_call(functools.partial(kernel, n_slab, n_sub, stages), out_shap...  43.7 us
    unnamed x2, local copies, waits for them, and re-layouts  1.76 us

profile of v2, /device:TPU:1, one launch (start us, length us, event | category | flops | bytes accessed | tf_op | source)
XLA Modules:
  0.0 46.1 jit_solution(4242898838180590465)
XLA Ops:
  0.6 43.7 %shard_map.86 = (f32[1536,128]{1,0:T(8,128)S(1)}, f32[1536,128]{1,0:T(8,128)S(1)}) custom-call(bf16[32,6,8,128]{3,2,1,0:T(8,128)(2,1)} %m_any.1, f32[6,8,128]{2,1,0:T(8,128)} %ss_any.1, f32[6,8,128]{2,1,0:T(8,128)} %cs_any.1, f32[8,128]{1,0:T(8,128)} %sg_any.1, f32[8,128]{1,0:T(8,128)} %cg_any.1, f32[6,8,128]{2,1,0:T(8,128)} %gr_any.1, s32[1024]{0:T(1024)} %len_any.1), custom_call_target="tpu_custom_call" | custom-call | tf_op jit(solution)/shard_map/pallas_call | solution.py:569
  44.3 0.9 %copy.11 = f32[32,6,8,128]{3,2,1,0:T(8,128)} copy(f32[32,6,8,128]{3,2,1,0:T(8,128)S(1)} %bitcast.3) | data formatting | bytes 1572864
  45.2 0.9 %copy.12 = f32[32,6,8,128]{3,2,1,0:T(8,128)} copy(f32[32,6,8,128]{3,2,1,0:T(8,128)S(1)} %bitcast.2) | data formatting | bytes 1572864

commit v3 on v2

--- a/solution.py
+++ b/solution.py
@@ -13,17 +13,18 @@
 M = 32
 GROUPS = 4
 GM = M // GROUPS
-UNROLL = 4
+UNROLL = 8
+
+
+def digits_of(n_slab):
+    core = 2
+    z = 16 if n_slab % 32 == 0 else 4 if n_slab % 8 == 0 else 1
+    return core, z, n_slab // (core * z)
 
 
 def digit_stages(n_slab, n_sub):
-    core = 2
-    z = 16 if n_slab % 32 == 0 else 1
-    y = n_slab // (core * z)
-    near = [("slab", 1, core), ("sub", 1, n_sub)]
-    if y > 1:
-        near.append(("slab", core * z, y))
-    return [near, [("slab", core, z)]] if z > 1 else [near]
+    core, z, y = digits_of(n_slab)
+    return [[("slab", 1, core), ("sub", 1, n_sub), ("slab", core * z, y)], [("slab", core, z)]]
 
 
 def stage_partners(digits, slab, sub):
@@ -64,8 +65,13 @@
     cg_any,
     gr_any,
     len_any,
-    x_ref,
-    r_ref,
+    r0,
+    z0,
+    q0,
+    d0,
+    image2,
+    over,
+    other,
     len_ref,
     m_in,
     ss,
@@ -74,10 +80,6 @@
     cg,
     gr,
     field,
-    r0,
-    z0,
-    q0,
-    d0,
     ssb,
     csb,
     fac,
@@ -110,7 +112,7 @@
     *rest,
 ):
     parts = rest[: len(stages)]
-    in_sem, send_sem, recv_sem = rest[len(stages) :]
+    in_sem, send_sem, recv_sem, here_sem = rest[len(stages) :]
     slab, sub = lax.axis_index("slab"), lax.axis_index("sub")
     ahead = (lax.rem(slab + 1, n_slab), sub)
     behind = (lax.rem(slab + n_slab - 1, n_slab), sub)
@@ -126,10 +128,31 @@
         copy.start()
         loads.append(copy)
 
+    core, z_size, y_size = digits_of(n_slab)
+    flat = stage_partners([("slab", 1, core), ("sub", 1, n_sub)], slab, sub)
+    ring_y = stage_partners([("slab", core * z_size, y_size)], slab, sub)
+    ring_z = stage_partners([("slab", core, z_size)], slab, sub)
+
+    def along_z(distance):
+        return [ring_z[distance - 1], ring_z[z_size - distance - 1]] if z_size > 1 else []
+
+    def tell(semaphore, devices):
+        for device in devices:
+            pl.semaphore_signal(semaphore, inc=1, device_id=device, device_id_type=MESH)
+
     barrier = pltpu.get_barrier_semaphore()
-    greeted = [ahead, behind, right, left] + [p for group in partners for p in group]
-    for device in greeted:
-        pl.semaphore_signal(barrier, inc=1, device_id=device, device_id_type=MESH)
+    greeted = [ahead, behind] + flat + ring_y + along_z(1)
+    tell(barrier, greeted)
+
+    reaches = [distance for distance in (1, 2, 4) if 2 * distance < z_size]
+    told = [0]
+
+    def widen():
+        if 0 < told[0] <= len(reaches):
+            pl.semaphore_wait(here_sem.at[told[0]], 2)
+        if told[0] < len(reaches):
+            tell(here_sem.at[told[0] + 1], along_z(reaches[told[0]]))
+        told[0] += 1
 
     row = lax.broadcasted_iota(jnp.int32, (R, C), 0)
     lane = lax.broadcasted_iota(jnp.int32, (R, C), 1)
@@ -211,6 +234,8 @@
     coef_send[1] = chord_coef
 
     pl.semaphore_wait(barrier, len(greeted))
+    tell(here_sem.at[0], flat)
+    widen()
     got_coef = [
         send(coef_send.at[0], coef_span, ahead),
         send(coef_send.at[1], coef_chord, right),
@@ -269,6 +294,7 @@
 
     for copy in got_coef:
         copy.wait_recv()
+    widen()
     chord_ghost = coef_chord[...]
     for c in range(D):
         mine = ss[c]
@@ -426,6 +452,7 @@
         prod[tile(2 * M + j), :] = total_of(a * b for a, b in zip(second, left_over))
         return dots(j, second, packed)
 
+    widen()
     got_second = []
     for g in range(GROUPS):
         for copy in got_first[g]:
@@ -444,7 +471,7 @@
     def second_step(edge, j, carry):
         second = of_mode(d0, j)
         image = operate(1, j, second, edge)
-        keep(field, j, image)
+        keep(image2, j, image)
         prod[tile(3 * M + j), :] = total_of(a * b for a, b in zip(second, image))
         return carry
 
@@ -455,6 +482,9 @@
     for k in range(3 * M // 8, 4 * M // 8):
         fold(k)
 
+    pl.semaphore_wait(here_sem.at[0], len(flat))
+    while told[0] <= len(reaches):
+        widen()
     own = jnp.sum(jnp.transpose(flip[...]), axis=0, keepdims=True)
     for part, group in zip(parts, partners):
         members = len(group) + 1
@@ -476,20 +506,13 @@
     second_part = (ds - dq * (zs / zq)) / (dv - ratio * dq)
     excess = (zs - dq * second_part) / zq
 
-    def last_step(j, carry):
-        turned = lax.rem(C - j, C)
-        over = wide(pltpu.roll(excess, turned, 1)[:, :1])
-        other = wide(pltpu.roll(second_part, turned, 1)[:, :1])
-        main = 1.0 + over
-        for c in range(D):
-            at = tile(j * D + c)
-            image = q0[at, :]
-            x_ref[at, :] = main * z0[at, :] + other * d0[at, :]
-            r_ref[at, :] = ((r0[at, :] - image) - over * image) - other * field[at, :]
+    def spread(j, carry):
+        over[tile(j), :] = wide(pltpu.roll(excess, C - 1 - j, 1)[:, C - 1 :])
+        other[tile(j), :] = wide(pltpu.roll(second_part, C - 1 - j, 1)[:, C - 1 :])
         return carry
 
     for g in range(GROUPS):
-        over_group(g, last_step, 0)
+        over_group(g, spread, 0)
     for copy in sent:
         copy.wait_send()
 
@@ -517,10 +540,6 @@
         pltpu.VMEM((R, C), f32),
         pltpu.VMEM((R, C), f32),
         pltpu.VMEM((D, R, C), f32),
-        big(),
-        big(),
-        big(),
-        big(),
         big(),
         pltpu.VMEM((D, R, C), f32),
         pltpu.VMEM((D, R, C), f32),
@@ -557,6 +576,7 @@
         pltpu.SemaphoreType.DMA((7,)),
         pltpu.SemaphoreType.DMA((n_sends,)),
         pltpu.SemaphoreType.DMA((n_sends,)),
+        pltpu.SemaphoreType.REGULAR((4,)),
     ]
     operands = [
         pltpu.with_memory_space_constraint(value, pltpu.HBM)
@@ -566,18 +586,22 @@
     ]
     in_hbm = pl.BlockSpec(memory_space=pltpu.HBM)
     shape = jax.ShapeDtypeStruct((M * D * R, C), f32)
-    adjoint, residual = pl.pallas_call(
+    per_mode = jax.ShapeDtypeStruct((M * R, C), f32)
+    in_vmem = pl.BlockSpec(memory_space=pltpu.VMEM)
+    fields = pl.pallas_call(
         functools.partial(kernel, n_slab, n_sub, stages),
-        out_shape=(shape, shape),
+        out_shape=(shape,) * 5 + (per_mode,) * 2,
         in_specs=[in_hbm] * 7,
-        out_specs=(pl.BlockSpec(memory_space=pltpu.VMEM),) * 2,
+        out_specs=(in_vmem,) * 7,
         scratch_shapes=scratch,
         compiler_params=pltpu.CompilerParams(
             collective_id=0, has_side_effects=True, vmem_limit_bytes=24 << 20
         ),
     )(*operands)
     full = (M, D, R, C)
-    return adjoint.reshape(full), residual.reshape(full)
+    r0, z0, q0, d0, image2 = [value.reshape(full) for value in fields[:5]]
+    over, other = [value.reshape(M, 1, R, C) for value in fields[5:]]
+    return z0 + over * z0 + other * d0, (r0 - q0) - over * q0 - other * image2
 
 
 def solution(mesh):

time: 46.2 us -> 41.7 us (0.903)
  Pallas kernels: 43.7 us -> 39.5 us
  local copies, waits for them, and re-layouts: 1.76 us -> 0 us
  other arithmetic: 0 us -> 1.44 us
    pallas_call x1, Pallas kernels: 43.7 us -> 39.5 us  [body(): pl.pallas_call(functools.partial(kernel, n_slab, n_sub, stages), out_shap...]
    unnamed x2 -> x0, local copies, waits for them, and re-layouts: 1.76 us -> none
    sub x0 -> x1, other arithmetic: none -> 1.44 us  [body(): return (z0 + over * z0 + other * d0, r0 - q0 - over * q0 - other * image2)]
where the time goes in v3:
time: 41.7 us; the launch traced here: 41.6 us
  Pallas kernels  39.5 us (95%)
  other arithmetic  1.44 us (3%)
  between operations  0.64 us (2%)
    pallas_call x1, Pallas kernels, body(): pl.pallas_call(functools.partial(kernel, n_slab, n_sub, stages), out_shap...  39.5 us
    sub x1, other arithmetic, body(): return (z0 + over * z0 + other * d0, r0 - q0 - over * q0 - other * image2)  1.44 us

profile of v3, /device:TPU:1, one launch (start us, length us, event | category | flops | bytes accessed | tf_op | source)
XLA Modules:
  0.0 41.6 jit_solution(5294380871011509062)
XLA Ops:
  0.6 39.5 %shard_map.86 = (f32[1536,128]{1,0:T(8,128)S(1)}, f32[1536,128]{1,0:T(8,128)S(1)}, f32[1536,128]{1,0:T(8,128)S(1)}, f32[1536,128]{1,0:T(8,128)S(1)}, f32[1536,12...) custom-call(bf16[32,6,8,128]{3,2,1,0:T(8,128)(2,1)} %m_any.1, f32[6,8,128]{2,1,0:T(8,128)} %ss_any.1, ...), custom_call_target="tpu_custom_call" | custom-call | tf_op jit(solution)/shard_map/pallas_call | solution.py:591
  40.2 1.4 %multiply_subtract_fusion = (f32[32,6,8,128]{3,2,1,0:T(8,128)}, f32[32,6,8,128]{3,2,1,0:T(8,128)}) fusion(f32[32,6,8,128]{3,2,1,0:T(8,128)S(1)} %bitcast.11, f32[32,6,8,128]{3,2,1,0:T(8,128)S(1)} %bitcast.9, f32[32,6,8,128]{3,2,1,0:T(8,128)S(1)} %bitcast.7, f32[32,8,128]{2,1,0:T(8,128)S(1)} %bitcast.13, f32[32,8,128]{2,1,0:T(8,128)S(1)} %bitcast.12, ...), kind=kLoop, calls=%fused_computation.2 | loop fusion | flops 1769472 | bytes 5767168 | tf_op jit(solution)/shard_map/sub | solution.py:604

commit v4 on v3

--- a/solution.py
+++ b/solution.py
@@ -11,9 +11,9 @@
 D = 6
 R, C = 8, 128
 M = 32
-GROUPS = 4
+GROUPS = 2
 GM = M // GROUPS
-UNROLL = 8
+UNROLL = 16
 
 
 def digits_of(n_slab):
@@ -125,33 +125,40 @@
         ((m_any, m_in), (ss_any, ss), (cs_any, cs), (sg_any, sg), (cg_any, cg), (gr_any, gr), (len_any, len_ref))
     ):
         copy = pltpu.make_async_copy(source, target, in_sem.at[k])
-        copy.start()
         loads.append(copy)
 
     core, z_size, y_size = digits_of(n_slab)
-    flat = stage_partners([("slab", 1, core), ("sub", 1, n_sub)], slab, sub)
+    ring_x = stage_partners([("sub", 1, n_sub)], slab, sub)
     ring_y = stage_partners([("slab", core * z_size, y_size)], slab, sub)
     ring_z = stage_partners([("slab", core, z_size)], slab, sub)
-
-    def along_z(distance):
-        return [ring_z[distance - 1], ring_z[z_size - distance - 1]] if z_size > 1 else []
+    twin = stage_partners([("slab", 1, core)], slab, sub)
+
+    def both_ways(ring, distance):
+        return [ring[distance - 1], ring[len(ring) - distance]] if ring else []
 
     def tell(semaphore, devices):
         for device in devices:
             pl.semaphore_signal(semaphore, inc=1, device_id=device, device_id_type=MESH)
 
     barrier = pltpu.get_barrier_semaphore()
-    greeted = [ahead, behind] + flat + ring_y + along_z(1)
+    greeted = [ahead, behind] + both_ways(ring_x, 1) + twin
+    greeted += both_ways(ring_y, 1) + both_ways(ring_z, 1)
     tell(barrier, greeted)
-
-    reaches = [distance for distance in (1, 2, 4) if 2 * distance < z_size]
+    for copy in loads:
+        copy.start()
+
+    steps = [
+        [both_ways(ring_x, 1), both_ways(ring_y, 1), both_ways(ring_y, 1), twin],
+        [both_ways(ring_z, distance) for distance in (1, 2, 4) if 2 * distance < z_size],
+    ]
     told = [0]
 
     def widen():
-        if 0 < told[0] <= len(reaches):
-            pl.semaphore_wait(here_sem.at[told[0]], 2)
-        if told[0] < len(reaches):
-            tell(here_sem.at[told[0] + 1], along_z(reaches[told[0]]))
+        for n, chain in enumerate(steps):
+            if 0 < told[0] <= len(chain) and chain[told[0] - 1]:
+                pl.semaphore_wait(here_sem.at[n, told[0] - 1], len(chain[told[0] - 1]))
+            if told[0] < len(chain):
+                tell(here_sem.at[n, told[0]], chain[told[0]])
         told[0] += 1
 
     row = lax.broadcasted_iota(jnp.int32, (R, C), 0)
@@ -234,7 +241,6 @@
     coef_send[1] = chord_coef
 
     pl.semaphore_wait(barrier, len(greeted))
-    tell(here_sem.at[0], flat)
     widen()
     got_coef = [
         send(coef_send.at[0], coef_span, ahead),
@@ -423,6 +429,7 @@
         keep(z0, j, first_z)
         return dots(j, first_z, packed)
 
+    widen()
     got_first = []
     for g in range(GROUPS):
         for b in range(GM // 8):
@@ -475,6 +482,7 @@
         prod[tile(3 * M + j), :] = total_of(a * b for a, b in zip(second, image))
         return carry
 
+    widen()
     for g in range(GROUPS):
         for copy in got_second[g]:
             copy.wait_recv()
@@ -482,8 +490,7 @@
     for k in range(3 * M // 8, 4 * M // 8):
         fold(k)
 
-    pl.semaphore_wait(here_sem.at[0], len(flat))
-    while told[0] <= len(reaches):
+    while told[0] <= 4:
         widen()
     own = jnp.sum(jnp.transpose(flip[...]), axis=0, keepdims=True)
     for part, group in zip(parts, partners):
@@ -576,7 +583,7 @@
         pltpu.SemaphoreType.DMA((7,)),
         pltpu.SemaphoreType.DMA((n_sends,)),
         pltpu.SemaphoreType.DMA((n_sends,)),
-        pltpu.SemaphoreType.REGULAR((4,)),
+        pltpu.SemaphoreType.REGULAR((2, 4)),
     ]
     operands = [
         pltpu.with_memory_space_constraint(value, pltpu.HBM)

time: 41.7 us -> 42.2 us (1.012)
  Pallas kernels: 39.5 us -> 40 us
    pallas_call x1, Pallas kernels: 39.5 us -> 40 us  [body(): pl.pallas_call(functools.partial(kernel, n_slab, n_sub, stages), out_shap...]
where the time goes in v4:
time: 42.2 us; the launch traced here: 42.1 us
  Pallas kernels  40 us (95%)
  other arithmetic  1.44 us (3%)
  between operations  0.64 us (2%)
    pallas_call x1, Pallas kernels, body(): pl.pallas_call(functools.partial(kernel, n_slab, n_sub, stages), out_shap...  40 us
    sub x1, other arithmetic, body(): return (z0 + over * z0 + other * d0, r0 - q0 - over * q0 - other * image2)  1.44 us

profile of v4, /device:TPU:1, one launch (start us, length us, event | category | flops | bytes accessed | tf_op | source)
XLA Modules:
  0.0 42.1 jit_solution(14702017457794527051)
XLA Ops:
  0.6 40.0 %shard_map.86 = (f32[1536,128]{1,0:T(8,128)S(1)}, f32[1536,128]{1,0:T(8,128)S(1)}, f32[1536,128]{1,0:T(8,128)S(1)}, f32[1536,128]{1,0:T(8,128)S(1)}, f32[1536,12...) custom-call(bf16[32,6,8,128]{3,2,1,0:T(8,128)(2,1)} %m_any.1, f32[6,8,128]{2,1,0:T(8,128)} %ss_any.1, ...), custom_call_target="tpu_custom_call" | custom-call | tf_op jit(solution)/shard_map/pallas_call | solution.py:598
  40.6 1.4 %multiply_subtract_fusion = (f32[32,6,8,128]{3,2,1,0:T(8,128)}, f32[32,6,8,128]{3,2,1,0:T(8,128)}) fusion(f32[32,6,8,128]{3,2,1,0:T(8,128)S(1)} %bitcast.11, f32[32,6,8,128]{3,2,1,0:T(8,128)S(1)} %bitcast.9, f32[32,6,8,128]{3,2,1,0:T(8,128)S(1)} %bitcast.7, f32[32,8,128]{2,1,0:T(8,128)S(1)} %bitcast.13, f32[32,8,128]{2,1,0:T(8,128)S(1)} %bitcast.12, ...), kind=kLoop, calls=%fused_computation.2 | loop fusion | flops 1769472 | bytes 5767168 | tf_op jit(solution)/shard_map/sub | solution.py:611

commit v5 on v4

--- a/solution.py
+++ b/solution.py
@@ -82,6 +82,13 @@
     field,
     ssb,
     csb,
+    edge_s,
+    edge_c,
+    back_s,
+    back_c,
+    cross,
+    hs,
+    hc,
     fac,
     ts,
     us,
@@ -350,16 +357,20 @@
     def solve(vector):
         return [total_of(fac[place(i, j)] * vector[j] for j in range(D)) for i in range(D)]
 
-    def dots(j, vector, packed):
-        t_s = total_of(ss[c] * vector[c] for c in range(D))
-        u_s = total_of(ssb[c] * vector[c] for c in range(D))
-        t_c = total_of(cs[c] * vector[c] for c in range(D))
-        u_c = total_of(csb[c] * vector[c] for c in range(D))
-        ts[tile(j), :] = t_s
-        us[tile(j), :] = u_s
-        tc[tile(j), :] = t_c
-        uc[tile(j), :] = u_c
-        turned = pltpu.roll(jnp.where(lane == 0, u_c, t_c), 2 * j + 1, 1)
+    def dots(vector):
+        return [
+            total_of(coef[c] * vector[c] for c in range(D)) for coef in (ss, ssb, cs, csb)
+        ]
+
+    def keep_dots(j, values):
+        for ref, value in zip((ts, us, tc, uc), values):
+            ref[tile(j), :] = value
+
+    def kept_dots(j):
+        return [ref[tile(j), :] for ref in (ts, us, tc, uc)]
+
+    def pack_dots(j, values, packed):
+        turned = pltpu.roll(jnp.where(lane == 0, values[3], values[2]), 2 * j + 1, 1)
         return jnp.where(pair == j, turned, packed)
 
     def send_dots(turn, g, packed):
@@ -384,20 +395,26 @@
             pltpu.roll(tu_behind[turn, g], 1, 1),
         )
 
-    def operate(turn, j, vector, edge):
-        t_s, u_s, t_c, u_c = ts[tile(j), :], us[tile(j), :], tc[tile(j), :], uc[tile(j), :]
-        at = pl.ds(turn * M + j, 1)
-        edge = pltpu.roll(edge, C - 1 - 2 * j, 1)
-        u_s_next = jnp.where(row == R - 1, wide(u_ahead[at, :]), pltpu.roll(u_s, R - 1, 0))
-        t_s_prev = jnp.where(row == 0, wide(t_behind[at, :]), pltpu.roll(t_s, 1, 0))
-        u_c_next = jnp.where(lane == C - 1, edge, pltpu.roll(u_c, C - 1, 1))
-        t_c_prev = jnp.where(lane == 0, edge, pltpu.roll(t_c, 1, 1))
+    def operate(vector, values):
+        t_s, u_s, t_c, u_c = values
+        u_s_next = jnp.where(row == R - 1, 0.0, pltpu.roll(u_s, R - 1, 0))
+        t_s_prev = jnp.where(row == 0, 0.0, pltpu.roll(t_s, 1, 0))
+        u_c_next = jnp.where(lane == C - 1, 0.0, pltpu.roll(u_c, C - 1, 1))
+        t_c_prev = jnp.where(lane == 0, 0.0, pltpu.roll(t_c, 1, 1))
         e_s, e_sb = u_s_next - t_s, u_s - t_s_prev
         e_c, e_cb = u_c_next - t_c, u_c - t_c_prev
         return [
             (gr[c] * vector[c] + (ssb[c] * e_sb - ss[c] * e_s)) + (csb[c] * e_cb - cs[c] * e_c)
             for c in range(D)
         ]
+
+    def arrived(turn, j, edge):
+        at = pl.ds(turn * M + j, 1)
+        along_s = jnp.where(row == 0, wide(t_behind[at, :]), wide(u_ahead[at, :]))
+        along_c = pltpu.roll(edge, C - 1 - 2 * j, 1)
+        hs[tile(j), :] = along_s
+        hc[tile(j), :] = along_c
+        return along_s, along_c
 
     for copy in got_cols:
         copy.wait_recv()
@@ -427,7 +444,9 @@
         first_z = solve(load)
         keep(r0, j, load)
         keep(z0, j, first_z)
-        return dots(j, first_z, packed)
+        values = dots(first_z)
+        keep_dots(j, values)
+        return pack_dots(j, values, packed)
 
     widen()
     got_first = []
@@ -447,26 +466,67 @@
             w_behind[pl.ds(block * 8, 8), :] = total_of(to_behind) * geo_behind
         got_first.append(send_dots(0, g, over_group(g, load_step, zero)))
 
+    for c in range(D):
+        edge_s[c] = jnp.where(row == R - 1, ss[c], jnp.where(row == 0, ssb[c], 0.0))
+        edge_c[c] = jnp.where(lane == C - 1, cs[c], jnp.where(lane == 0, csb[c], 0.0))
+    for source, target in ((edge_s, back_s), (edge_c, back_c)):
+        for c, value in enumerate(solve([source[c] for c in range(D)])):
+            target[c] = value
+    for n, source in enumerate((back_s, back_c)):
+        for k, value in enumerate(dots([source[c] for c in range(D)])):
+            cross[2 * k + n] = value
+
+    def base_step(j, carry):
+        z = of_mode(z0, j)
+        image = operate(z, kept_dots(j))
+        second = solve([a - b for a, b in zip(of_mode(r0, j), image)])
+        keep(q0, j, image)
+        keep(d0, j, second)
+        keep_dots(j, dots(second))
+        return carry
+
+    for g in range(GROUPS):
+        over_group(g, base_step, 0)
+    widen()
+
     def first_step(edge, j, packed):
-        z = of_mode(z0, j)
-        image = operate(0, j, z, edge)
+        along_s, along_c = arrived(0, j, edge)
+        values = [
+            value + (cross[2 * k] * along_s + cross[2 * k + 1] * along_c)
+            for k, value in enumerate(kept_dots(j))
+        ]
+        keep_dots(j, values)
+        return pack_dots(j, values, packed)
+
+    got_second = []
+    for g in range(GROUPS):
+        for copy in got_first[g]:
+            copy.wait_recv()
+        packed = over_group(g, functools.partial(first_step, edges_of(0, g)), zero)
+        got_second.append(send_dots(1, g, packed))
+
+    def finish_step(j, carry):
+        along_s, along_c = hs[tile(j), :], hc[tile(j), :]
+        z, image, second = of_mode(z0, j), of_mode(q0, j), of_mode(d0, j)
+        image = [
+            value - (edge_s[c] * along_s + edge_c[c] * along_c) for c, value in enumerate(image)
+        ]
+        second = [
+            value + (back_s[c] * along_s + back_c[c] * along_c) for c, value in enumerate(second)
+        ]
         left_over = [a - b for a, b in zip(of_mode(r0, j), image)]
-        second = solve(left_over)
         keep(q0, j, image)
         keep(d0, j, second)
         prod[tile(j), :] = total_of(a * b for a, b in zip(z, image))
         prod[tile(M + j), :] = total_of(a * b for a, b in zip(z, left_over))
         prod[tile(2 * M + j), :] = total_of(a * b for a, b in zip(second, left_over))
-        return dots(j, second, packed)
-
-    widen()
-    got_second = []
+        image = operate(second, kept_dots(j))
+        keep(image2, j, image)
+        prod[tile(3 * M + j), :] = total_of(a * b for a, b in zip(second, image))
+        return carry
+
     for g in range(GROUPS):
-        for copy in got_first[g]:
-            copy.wait_recv()
-        edge = edges_of(0, g)
-        packed = over_group(g, functools.partial(first_step, edge), zero)
-        got_second.append(send_dots(1, g, packed))
+        over_group(g, finish_step, 0)
 
     def fold(k):
         rows = [prod[pl.ds(k * 8 * R + n, 8, stride=R), :] for n in range(R)]
@@ -474,21 +534,31 @@
 
     for k in range(3 * M // 8):
         fold(k)
+    widen()
 
     def second_step(edge, j, carry):
-        second = of_mode(d0, j)
-        image = operate(1, j, second, edge)
-        keep(image2, j, image)
-        prod[tile(3 * M + j), :] = total_of(a * b for a, b in zip(second, image))
+        along_s, along_c = arrived(1, j, edge)
+        t_s, u_s, t_c, u_c = kept_dots(j)
+        change = jnp.where(row == R - 1, t_s, jnp.where(row == 0, u_s, 0.0)) * along_s
+        change = change + (
+            jnp.where(lane == C - 1, t_c, jnp.where(lane == 0, u_c, 0.0)) * along_c
+        )
+        prod[tile(3 * M + j), :] = prod[tile(3 * M + j), :] - change
         return carry
 
-    widen()
     for g in range(GROUPS):
         for copy in got_second[g]:
             copy.wait_recv()
         over_group(g, functools.partial(second_step, edges_of(1, g)), 0)
     for k in range(3 * M // 8, 4 * M // 8):
         fold(k)
+
+    def last_image(j, carry):
+        along_s, along_c = hs[tile(j), :], hc[tile(j), :]
+        for c in range(D):
+            at = tile(j * D + c)
+            image2[at, :] = image2[at, :] - (edge_s[c] * along_s + edge_c[c] * along_c)
+        return carry
 
     while told[0] <= 4:
         widen()
@@ -500,6 +570,9 @@
             send(part.at[pl.ds(0, 1)], part.at[pl.ds(n + 1, 1)], device)
             for n, device in enumerate(group)
         ]
+        if part is parts[0]:
+            for g in range(GROUPS):
+                over_group(g, last_image, 0)
         for copy in copies:
             copy.wait_recv()
         own = jnp.sum(part[pl.ds(0, members), :], axis=0, keepdims=True)
@@ -550,6 +623,13 @@
         big(),
         pltpu.VMEM((D, R, C), f32),
         pltpu.VMEM((D, R, C), f32),
+        pltpu.VMEM((D, R, C), f32),
+        pltpu.VMEM((D, R, C), f32),
+        pltpu.VMEM((D, R, C), f32),
+        pltpu.VMEM((D, R, C), f32),
+        pltpu.VMEM((8, R, C), f32),
+        pltpu.VMEM((M * R, C), f32),
+        pltpu.VMEM((M * R, C), f32),
         pltpu.VMEM((21, R, C), f32),
         pltpu.VMEM((M * R, C), f32),
         pltpu.VMEM((M * R, C), f32),

time: 42.2 us -> 41.8 us (level)
    pallas_call x1, Pallas kernels: 40 us -> 39.6 us  [body(): pl.pallas_call(functools.partial(kernel, n_slab, n_sub, stages), out_shap...]
where the time goes in v5:
time: 41.8 us; the launch traced here: 41.6 us
  Pallas kernels  39.6 us (95%)
  other arithmetic  1.44 us (3%)
  between operations  0.64 us (2%)
    pallas_call x1, Pallas kernels, body(): pl.pallas_call(functools.partial(kernel, n_slab, n_sub, stages), out_shap...  39.6 us
    sub x1, other arithmetic, body(): return (z0 + over * z0 + other * d0, r0 - q0 - over * q0 - other * image2)  1.44 us

profile of v5, /device:TPU:1, one launch (start us, length us, event | category | flops | bytes accessed | tf_op | source)
XLA Modules:
  0.0 41.6 jit_solution(8047032539901586276)
XLA Ops:
  0.6 39.6 %shard_map.86 = (f32[1536,128]{1,0:T(8,128)S(1)}, f32[1536,128]{1,0:T(8,128)S(1)}, f32[1536,128]{1,0:T(8,128)S(1)}, f32[1536,128]{1,0:T(8,128)S(1)}, f32[1536,12...) custom-call(bf16[32,6,8,128]{3,2,1,0:T(8,128)(2,1)} %m_any.1, f32[6,8,128]{2,1,0:T(8,128)} %ss_any.1, ...), custom_call_target="tpu_custom_call" | custom-call | tf_op jit(solution)/shard_map/pallas_call | solution.py:678
  40.2 1.4 %multiply_subtract_fusion = (f32[32,6,8,128]{3,2,1,0:T(8,128)}, f32[32,6,8,128]{3,2,1,0:T(8,128)}) fusion(f32[32,6,8,128]{3,2,1,0:T(8,128)S(1)} %bitcast.11, f32[32,6,8,128]{3,2,1,0:T(8,128)S(1)} %bitcast.9, f32[32,6,8,128]{3,2,1,0:T(8,128)S(1)} %bitcast.7, f32[32,8,128]{2,1,0:T(8,128)S(1)} %bitcast.13, f32[32,8,128]{2,1,0:T(8,128)S(1)} %bitcast.12, ...), kind=kLoop, calls=%fused_computation.2 | loop fusion | flops 1769472 | bytes 5767168 | tf_op jit(solution)/shard_map/sub | solution.py:691

commit v6 on v5

--- a/solution.py
+++ b/solution.py
@@ -158,15 +158,15 @@
         [both_ways(ring_x, 1), both_ways(ring_y, 1), both_ways(ring_y, 1), twin],
         [both_ways(ring_z, distance) for distance in (1, 2, 4) if 2 * distance < z_size],
     ]
-    told = [0]
-
-    def widen():
-        for n, chain in enumerate(steps):
-            if 0 < told[0] <= len(chain) and chain[told[0] - 1]:
-                pl.semaphore_wait(here_sem.at[n, told[0] - 1], len(chain[told[0] - 1]))
-            if told[0] < len(chain):
-                tell(here_sem.at[n, told[0]], chain[told[0]])
-        told[0] += 1
+    told = [0, 0]
+
+    def widen(n):
+        chain, step = steps[n], told[n]
+        if 0 < step <= len(chain) and chain[step - 1]:
+            pl.semaphore_wait(here_sem.at[n, step - 1], len(chain[step - 1]))
+        if step < len(chain):
+            tell(here_sem.at[n, step], chain[step])
+        told[n] += 1
 
     row = lax.broadcasted_iota(jnp.int32, (R, C), 0)
     lane = lax.broadcasted_iota(jnp.int32, (R, C), 1)
@@ -248,7 +248,8 @@
     coef_send[1] = chord_coef
 
     pl.semaphore_wait(barrier, len(greeted))
-    widen()
+    widen(0)
+    widen(1)
     got_coef = [
         send(coef_send.at[0], coef_span, ahead),
         send(coef_send.at[1], coef_chord, right),
@@ -307,7 +308,8 @@
 
     for copy in got_coef:
         copy.wait_recv()
-    widen()
+    widen(0)
+    widen(1)
     chord_ghost = coef_chord[...]
     for c in range(D):
         mine = ss[c]
@@ -448,7 +450,6 @@
         keep_dots(j, values)
         return pack_dots(j, values, packed)
 
-    widen()
     got_first = []
     for g in range(GROUPS):
         for b in range(GM // 8):
@@ -487,7 +488,8 @@
 
     for g in range(GROUPS):
         over_group(g, base_step, 0)
-    widen()
+    widen(0)
+    widen(1)
 
     def first_step(edge, j, packed):
         along_s, along_c = arrived(0, j, edge)
@@ -534,7 +536,7 @@
 
     for k in range(3 * M // 8):
         fold(k)
-    widen()
+    widen(0)
 
     def second_step(edge, j, carry):
         along_s, along_c = arrived(1, j, edge)
@@ -560,11 +562,12 @@
             image2[at, :] = image2[at, :] - (edge_s[c] * along_s + edge_c[c] * along_c)
         return carry
 
-    while told[0] <= 4:
-        widen()
+    widen(0)
     own = jnp.sum(jnp.transpose(flip[...]), axis=0, keepdims=True)
     for part, group in zip(parts, partners):
         members = len(group) + 1
+        if part is not parts[0]:
+            widen(1)
         part[pl.ds(0, 1), :] = own
         copies = [
             send(part.at[pl.ds(0, 1)], part.at[pl.ds(n + 1, 1)], device)

time: 41.8 us -> 40.5 us (0.969)
  Pallas kernels: 39.6 us -> 38.3 us
    pallas_call x1, Pallas kernels: 39.6 us -> 38.3 us  [body(): pl.pallas_call(functools.partial(kernel, n_slab, n_sub, stages), out_shap...]
where the time goes in v6:
time: 40.5 us; the launch traced here: 40.4 us
  Pallas kernels  38.3 us (95%)
  other arithmetic  1.44 us (4%)
  between operations  0.64 us (2%)
    pallas_call x1, Pallas kernels, body(): pl.pallas_call(functools.partial(kernel, n_slab, n_sub, stages), out_shap...  38.3 us
    sub x1, other arithmetic, body(): return (z0 + over * z0 + other * d0, r0 - q0 - over * q0 - other * image2)  1.44 us

profile of v6, /device:TPU:1, one launch (start us, length us, event | category | flops | bytes accessed | tf_op | source)
XLA Modules:
  0.0 40.4 jit_solution(7972385750933652618)
XLA Ops:
  0.6 38.3 %shard_map.86 = (f32[1536,128]{1,0:T(8,128)S(1)}, f32[1536,128]{1,0:T(8,128)S(1)}, f32[1536,128]{1,0:T(8,128)S(1)}, f32[1536,128]{1,0:T(8,128)S(1)}, f32[1536,12...) custom-call(bf16[32,6,8,128]{3,2,1,0:T(8,128)(2,1)} %m_any.1, f32[6,8,128]{2,1,0:T(8,128)} %ss_any.1, ...), custom_call_target="tpu_custom_call" | custom-call | tf_op jit(solution)/shard_map/pallas_call | solution.py:681
  39.0 1.4 %multiply_subtract_fusion = (f32[32,6,8,128]{3,2,1,0:T(8,128)}, f32[32,6,8,128]{3,2,1,0:T(8,128)}) fusion(f32[32,6,8,128]{3,2,1,0:T(8,128)S(1)} %bitcast.11, f32[32,6,8,128]{3,2,1,0:T(8,128)S(1)} %bitcast.9, f32[32,6,8,128]{3,2,1,0:T(8,128)S(1)} %bitcast.7, f32[32,8,128]{2,1,0:T(8,128)S(1)} %bitcast.13, f32[32,8,128]{2,1,0:T(8,128)S(1)} %bitcast.12, ...), kind=kLoop, calls=%fused_computation.2 | loop fusion | flops 1769472 | bytes 5767168 | tf_op jit(solution)/shard_map/sub | solution.py:694

commit v7 on v6

--- a/solution.py
+++ b/solution.py
@@ -40,6 +40,22 @@
             at[axis] = at[axis] + ((digit + step) % size - digit) * stride
         partners.append((at["slab"], at["sub"]))
     return partners
+
+
+def farthest_first(digits):
+    total = 1
+    for _, _, size in digits:
+        total *= size
+
+    def hops(offset):
+        way, rest = 0, offset + 1
+        for axis, stride, size in digits:
+            step, rest = rest % size, rest // size
+            if (axis, stride) != ("slab", 1):
+                way += min(step, size - step)
+        return way
+
+    return sorted(range(total - 1), key=lambda offset: -hops(offset))
 
 
 def total_of(terms):
@@ -564,14 +580,14 @@
 
     widen(0)
     own = jnp.sum(jnp.transpose(flip[...]), axis=0, keepdims=True)
-    for part, group in zip(parts, partners):
+    for part, group, digits in zip(parts, partners, stages):
         members = len(group) + 1
         if part is not parts[0]:
             widen(1)
         part[pl.ds(0, 1), :] = own
         copies = [
-            send(part.at[pl.ds(0, 1)], part.at[pl.ds(n + 1, 1)], device)
-            for n, device in enumerate(group)
+            send(part.at[pl.ds(0, 1)], part.at[pl.ds(n + 1, 1)], group[n])
+            for n in farthest_first(digits)
         ]
         if part is parts[0]:
             for g in range(GROUPS):

time: 40.5 us -> 40.4 us (level)
  no operation moved by 1% of the time
where the time goes in v7:
time: 40.4 us; the launch traced here: 40.3 us
  Pallas kernels  38.2 us (95%)
  other arithmetic  1.44 us (4%)
  between operations  0.64 us (2%)
    pallas_call x1, Pallas kernels, body(): pl.pallas_call(functools.partial(kernel, n_slab, n_sub, stages), out_shap...  38.2 us
    sub x1, other arithmetic, body(): return (z0 + over * z0 + other * d0, r0 - q0 - over * q0 - other * image2)  1.44 us

profile of v7, /device:TPU:1, one launch (start us, length us, event | category | flops | bytes accessed | tf_op | source)
XLA Modules:
  0.0 40.3 jit_solution(16402012954816562593)
XLA Ops:
  0.6 38.2 %shard_map.86 = (f32[1536,128]{1,0:T(8,128)S(1)}, f32[1536,128]{1,0:T(8,128)S(1)}, f32[1536,128]{1,0:T(8,128)S(1)}, f32[1536,128]{1,0:T(8,128)S(1)}, f32[1536,12...) custom-call(bf16[32,6,8,128]{3,2,1,0:T(8,128)(2,1)} %m_any.1, f32[6,8,128]{2,1,0:T(8,128)} %ss_any.1, ...), custom_call_target="tpu_custom_call" | custom-call | tf_op jit(solution)/shard_map/pallas_call | solution.py:697
  38.8 1.4 %multiply_subtract_fusion = (f32[32,6,8,128]{3,2,1,0:T(8,128)}, f32[32,6,8,128]{3,2,1,0:T(8,128)}) fusion(f32[32,6,8,128]{3,2,1,0:T(8,128)S(1)} %bitcast.11, f32[32,6,8,128]{3,2,1,0:T(8,128)S(1)} %bitcast.9, f32[32,6,8,128]{3,2,1,0:T(8,128)S(1)} %bitcast.7, f32[32,8,128]{2,1,0:T(8,128)S(1)} %bitcast.13, f32[32,8,128]{2,1,0:T(8,128)S(1)} %bitcast.12, ...), kind=kLoop, calls=%fused_computation.2 | loop fusion | flops 1769472 | bytes 5767168 | tf_op jit(solution)/shard_map/sub | solution.py:710
